TPU v7x, 32 devices: a whole 2x2x4 slice. The times are simulated.
32 devices in a mesh: grp: 4 (over y, x), shard: 8 (over z, core).
Axes of the slice: x: 2, y: 2, z: 4, core: 2. Of those that a mesh axis runs over, the one named last changes fastest.
Arguments:
- embeddings: bfloat16 [2048, 1280], P('shard'), may hold values from -6 to 6
- w_in: bfloat16 [1280, 2048], P('shard', 'grp'), may hold values from -0.15625 to 0.15625
- bias: bfloat16 [2048], P('grp'), may hold values from -3 to 3
- w_out: bfloat16 [2048], P('grp'), may hold values from -0.125 to 0.125
- pair_left: int32 [16384], P('shard'), may hold values from 0 to 255
- pair_home: int32 [16384, 1], P('shard'), may hold values from 0 to 7; in each aligned block of 2048 rows (0 to 2047, 2048 to 4095, ...) at most 512 rows name the same one
- pair_remote: int32 [16384], P('shard'), may hold values from 0 to 255
- outcome: int32 [16384], P('shard'), may hold values from 0 to 1
Outputs:
- grad_weight: float32 [1280, 2048], P('shard', 'grp')
- head_grads: float32 [2048, 2], P(('grp', 'shard'))
Inputs may be any that keep to these rules, and one draw needn't show every extreme that they name: `pair_home`: among the pairs of one owner at most 512 have their second variant on one given index of shard, and in every draw some owner has exactly 512 with one index.
All inputs are finite; a program needn't handle non-finite values.
Results may differ from a plain program's by a relative error of at most 0.0016.
Values may be sent and summed in bfloat16 or wider, within the bound.
No kernel may reach another device: no remote copies, remote signals or barrier semaphores. Data moves between devices by JAX's collectives and lax.ppermute only.
A program may use at most 64 MiB of HBM per device.

v0:
```python
import functools

import jax
import jax.numpy as jnp
from jax import lax
from jax.experimental import pallas as pl
from jax.experimental.pallas import tpu as pltpu
from jax.sharding import PartitionSpec as P


F32 = jnp.float32
BF16 = jnp.bfloat16
LANES = 128
TAIL = 8
NT = (((1,), (1,)), ((), ()))


def activate(values):
    return jax.nn.gelu(values, approximate=True)


def vmem():
    return pl.BlockSpec(memory_space=pltpu.VMEM)


def call(body, inputs, outputs, scratch=(), flops=0, space=pltpu.VMEM):
    return pl.pallas_call(
        body,
        out_shape=outputs,
        in_specs=[pl.BlockSpec(memory_space=space)] * len(inputs),
        out_specs=[vmem()] * len(outputs),
        scratch_shapes=scratch,
        cost_estimate=pl.CostEstimate(flops=flops, bytes_accessed=1 << 20, transcendentals=0),
        compiler_params=pltpu.CompilerParams(vmem_limit_bytes=24 << 20),
    )(*inputs)


def pair_rows(ref, owner, part, chunk):
    return ref[owner, part, pl.ds(chunk, 1), :].astype(jnp.int32)


def transpose_kernel(own, partner, out):
    core = lax.axis_index("shard") % 2
    rows = own.shape[0]
    for j, ref in enumerate((own, partner)):
        at = pl.multiple_of((core ^ j) * rows, rows)
        out[:, pl.ds(at, rows)] = ref[...].T


def count_kernel(own, pairs, out, lefts):
    shard = lax.axis_index("shard")
    rows = out.shape[0]
    owners, _, chunks, _ = pairs.shape
    ids = lax.broadcasted_iota(jnp.int32, (rows, LANES), 0).astype(BF16)
    nought = jnp.zeros((), BF16)

    def table(ref, owner, home=None, sums=False):
        columns, added = [], jnp.zeros((rows, LANES), BF16)
        for q in range(chunks):
            row = pair_rows(ref, owner, 0, q)
            if home is not None:
                row = jnp.where(pair_rows(ref, owner, 1, q) == home, pair_rows(ref, owner, 2, q), -1)
            hit = ids == row.astype(BF16)
            columns.append(jnp.where(hit, jnp.ones((), BF16), nought).astype(jnp.float8_e5m2))
            if sums:
                half = jnp.where(pair_rows(ref, owner, 3, q) == 1, -0.5, 0.5).astype(BF16)
                added = added + jnp.where(hit, half, nought)
        return jnp.concatenate(columns, axis=1), added.astype(F32)

    lefts[...], total = table(own, 0, sums=True)
    for o in range(owners):
        here, _ = table(own, 0, home=o)
        there, added = table(pairs, o, home=shard, sums=True)
        theirs, _ = table(pairs, o)
        total = total - added
        out[:, o * rows : (o + 1) * rows] = 0.5 * (
            lax.dot_general(lefts[...], here, NT, preferred_element_type=F32)
            + lax.dot_general(there, theirs, NT, preferred_element_type=F32)
        )
    out[:, owners * rows :] = total


def forward_kernel(*refs):
    own, partner, bias, w_out = refs[:4]
    score, hidden, slope, gathered = refs[-4:]
    blocks = refs[4:-4]
    shard = lax.axis_index("shard")
    core = shard % 2
    rows = own.shape[0]
    depth = blocks[0].shape[0]
    half = hidden.shape[1]
    lane = pl.multiple_of(core * half, half)
    for m, ref in enumerate(blocks):
        at = pl.multiple_of((shard ^ m) * depth, depth)
        gathered[pl.ds(at, depth), :] = ref[:, pl.ds(lane, half)]
    shift = bias[:, pl.ds(lane, half)].astype(F32)
    weights = w_out[:, pl.ds(lane, half)]
    for j, ref in enumerate((own, partner)):
        at = pl.multiple_of((core ^ j) * rows, rows)
        pre = jnp.dot(ref[...], gathered[...], preferred_element_type=F32) + shift
        square = pre * pre
        scale = 0.7978845608028654
        t = jnp.tanh(scale * (pre + 0.044715 * (square * pre)))
        out = (pre * (0.5 * (1.0 + t))).astype(BF16)
        hidden[pl.ds(at, rows), :] = out
        slope[pl.ds(at, rows), :] = 0.5 * (1.0 + t) + (0.5 * pre) * (1.0 - t * t) * (
            scale * (1.0 + (3.0 * 0.044715) * square)
        )
        part = lax.dot_general(
            jnp.broadcast_to(weights, (8, half)), out, NT, preferred_element_type=F32
        )
        tiles = rows // LANES
        for q in range(tiles):
            piece = jnp.broadcast_to(part[0:1, q * LANES : (q + 1) * LANES], (score.shape[0], LANES))
            score[:, pl.ds((core ^ j) * tiles + q, 1), :] = piece.reshape(score.shape[0], 1, LANES)


def exponent_of(largest, limit):
    return jnp.maximum(jnp.ceil(jnp.log2(jnp.maximum(largest, 1e-30) * (1.0 / limit))), -100.0)


def coded(values):
    power = exponent_of(jnp.abs(values), 16000.0)
    scaled = values * jnp.exp2(-power)
    high = jnp.round(scaled)
    low = jnp.round((scaled - high) * 32000.0)
    return [power, high, low]


def decoded(rows, at):
    return (rows[at + 1 : at + 2, :] + rows[at + 2 : at + 3, :] * (1.0 / 32000.0)) * jnp.exp2(rows[at : at + 1, :])


def pair_kernel(groups, received, counts, dscore):
    shard = lax.axis_index("shard")
    rows = counts.shape[0]
    n = (counts.shape[1] - LANES) // rows
    tiles = rows // LANES

    def scores_of(s):
        z, j = s // 2, s % 2
        parts = [
            received[g * n + 2 * z + k, pl.ds(j * tiles, tiles), :] for g in range(groups) for k in range(2)
        ]
        while len(parts) > 1:
            parts = [a + b for a, b in zip(parts[::2], parts[1::2])]
        return parts[0] * 0.5

    across = [scores_of(s) for s in range(n)]
    turned = jnp.concatenate([scores_of(shard), jnp.zeros((8 - tiles, LANES), F32)], axis=0).T
    for q in range(tiles):
        span = slice(q * LANES, (q + 1) * LANES)
        column = jnp.broadcast_to(turned[:, q : q + 1], (LANES, LANES))
        total = counts[span, n * rows :]
        for s in range(n):
            for p in range(tiles):
                at = (s * tiles + p) * LANES
                total = total + counts[span, at : at + LANES] * jnp.tanh(column - across[s][p : p + 1, :])
        dscore[span, :] = jnp.sum(total, axis=1, keepdims=True)


def gradient_kernel(*refs):
    near, next_to, flipped, hidden, slope, w_out = refs[:6]
    kept, heads = refs[6:8]
    messages = refs[8:-2]
    terms, sent = refs[-2:]
    shard = lax.axis_index("shard")
    core = shard % 2
    rows = near.shape[0]
    half = hidden.shape[1]
    depth = kept.shape[0]
    lane = pl.multiple_of(core * half, half)
    weights = w_out[:, pl.ds(lane, half)].astype(F32)
    bias_sum = jnp.zeros((1, half), F32)
    score_sum = jnp.zeros((1, half), F32)
    for j, ref in enumerate((near, next_to)):
        for r in range(rows // LANES):
            there = pl.ds(pl.multiple_of((core ^ j) * rows + r * LANES, LANES), LANES)
            dscore = ref[r * LANES : (r + 1) * LANES, :]
            dpre = (dscore * weights) * slope[there, :]
            bias_sum = bias_sum + jnp.sum(dpre, axis=0, keepdims=True)
            score_sum = score_sum + jnp.sum(dscore * hidden[there, :].astype(F32), axis=0, keepdims=True)
            sent[there, :] = dpre.astype(BF16)
    terms[...] = jnp.dot(flipped[...], sent[...], preferred_element_type=F32)
    kept[...] = terms[pl.ds(pl.multiple_of(shard * depth, depth), depth), :]
    heads[...] = jnp.concatenate([bias_sum, score_sum], axis=0)
    extra = coded(bias_sum) + coded(score_sum)
    for m, ref in enumerate(messages, 1):
        block = terms[pl.ds(pl.multiple_of((shard ^ m) * depth, depth), depth), :]
        power = exponent_of(jnp.max(jnp.abs(block), axis=0, keepdims=True), 32000.0)
        ref[:depth, :] = jnp.round(block * jnp.exp2(-power)).astype(jnp.int32).astype(jnp.int16)
        pad = jnp.zeros((TAIL - 1 - len(extra), half), F32)
        tail = jnp.concatenate([power] + extra + [pad], axis=0)
        ref[depth:, :] = tail.astype(jnp.int32).astype(jnp.int16)


def sum_kernel(*refs):
    kept, heads = refs[:2]
    messages = refs[2:-2]
    weight, head = refs[-2:]
    shard = lax.axis_index("shard")
    core = shard % 2
    depth, half = kept.shape
    sums = [kept[...], jnp.zeros_like(kept)]
    tops = [heads[...], jnp.zeros_like(heads)]
    for m, ref in enumerate(messages, 1):
        tail = ref[depth:, :].astype(jnp.int32).astype(F32)
        sums[m % 2] = sums[m % 2] + ref[:depth, :].astype(jnp.int32).astype(F32) * jnp.exp2(tail[0:1, :])
        tops[m % 2] = tops[m % 2] + jnp.concatenate([decoded(tail, 1), decoded(tail, 4)], axis=0)
    weight[:, pl.ds(pl.multiple_of(core * half, half), half)] = sums[0]
    weight[:, pl.ds(pl.multiple_of((1 - core) * half, half), half)] = sums[1]
    units = head.shape[1]
    first = shard * units
    chosen = jnp.where(first // half == core, tops[0], tops[1])
    chosen = jnp.concatenate([chosen, jnp.zeros((6, half), F32)], axis=0)
    head[...] = pltpu.roll(chosen, (half - first % half) % half, 1)[:2, :units]


def by_ppermute(embeddings, w_in, bias, w_out, pair_left, pair_home, pair_remote, outcome):
    rows, channels = embeddings.shape
    depth, hidden_units = w_in.shape
    half = hidden_units // 2
    n = lax.axis_size("shard")
    groups = lax.axis_size("grp")
    pair_count = pair_left.shape[0]
    chunks = pair_count // LANES

    def swap(value, m):
        return lax.ppermute(value, "shard", [(i, i ^ m) for i in range(n)])

    far = range(n - 2, 0, -2)

    def spread(value):
        got = {0: value}
        for m in far:
            got[m] = swap(value, m)
        for m in (0, *far):
            got[m + 1] = swap(got[m], 1)
        return [got[m] for m in range(n)]

    blocks = spread(w_in)
    tile = (1, 1, chunks, LANES)
    columns = [a.reshape(tile) for a in (pair_left, pair_home, pair_remote, outcome)]
    part = lax.broadcasted_iota(jnp.int32, (n, 4, chunks, LANES), 1)
    pairs = columns[3]
    for k in (2, 1, 0):
        pairs = jnp.where(part == k, columns[k], pairs)
    pairs = pairs.astype(jnp.int16)
    lists = lax.all_to_all(pairs, "shard", 0, 0, tiled=True)
    partner = swap(embeddings, 1)
    shape = jax.ShapeDtypeStruct
    (flipped,) = call(transpose_kernel, (embeddings, partner), [shape((channels, 2 * rows), BF16)])
    (counts,) = call(
        count_kernel,
        (pairs, lists),
        [shape((rows, n * rows + LANES), F32)],
        [pltpu.VMEM((rows, pair_count), jnp.float8_e5m2)],
        flops=4 * rows * n * rows * pair_count,
    )
    bias, w_out = bias.reshape(1, -1), w_out.reshape(1, -1)
    score, hidden, slope = call(
        forward_kernel,
        (embeddings, partner, bias, w_out, *blocks),
        [
            shape((groups * n, 2 * rows // LANES, LANES), F32),
            shape((2 * rows, half), BF16),
            shape((2 * rows, half), F32),
        ],
        [pltpu.VMEM((channels, half), BF16)],
        flops=4 * rows * channels * half,
    )
    received = lax.all_to_all(score, ("grp", "shard"), 0, 0, tiled=True)
    (near,) = call(
        functools.partial(pair_kernel, groups), (received, counts), [shape((rows, 1), F32)], flops=rows * n * rows
    )
    next_to = swap(near, 1)
    message = shape((depth + TAIL, half), jnp.int16)
    kept, heads, *messages = call(
        gradient_kernel,
        (near, next_to, flipped, hidden, slope, w_out),
        [shape((depth, half), F32), shape((2, half), F32)] + [message] * (n - 1),
        [pltpu.VMEM((channels, half), F32), pltpu.VMEM((2 * rows, half), BF16)],
        flops=4 * rows * channels * half,
    )
    order = sorted(range(1, n), key=lambda m: -(m // 2))
    got = {m: swap(messages[m - 1], m) for m in order}
    weight, head = call(
        sum_kernel,
        (kept, heads, *[got[m] for m in range(1, n)]),
        [shape((depth, hidden_units), F32), shape((2, hidden_units // n), F32)],
    )
    return weight, head.T


def by_collectives(embeddings, w_in, bias, w_out, pair_left, pair_home, pair_remote, outcome):
    local_rows = embeddings.shape[0]
    devices = lax.axis_size("shard")
    pair_count = pair_left.shape[0]
    capacity = 2 * pair_count // devices
    pre = jnp.dot(
        embeddings,
        lax.all_gather(w_in, "shard", axis=0, tiled=True),
        preferred_element_type=jnp.float32,
    )
    pre = pre + bias.astype(jnp.float32)[None, :]
    hidden = activate(pre).astype(jnp.bfloat16)
    part_score = jnp.dot(hidden, w_out, preferred_element_type=jnp.float32)
    score = lax.psum(part_score, "grp")
    home_dev = pair_home[:, 0]
    onehot = (home_dev[:, None] == jnp.arange(devices, dtype=jnp.int32)[None, :]).astype(jnp.int32)
    slot_index = jnp.sum(jnp.cumsum(onehot, axis=0) * onehot, axis=1) - 1
    request = jnp.zeros((devices, capacity), jnp.int32).at[home_dev, slot_index].set(pair_remote)
    wanted = lax.all_to_all(request, "shard", split_axis=0, concat_axis=0, tiled=True)
    wanted_rows = wanted.reshape(-1)
    outgoing = score[wanted_rows].reshape(devices, capacity)
    remote_score = lax.all_to_all(outgoing, "shard", split_axis=0, concat_axis=0, tiled=True)
    margin = score[pair_left] - remote_score[home_dev, slot_index]
    resid = jax.nn.sigmoid(margin) - outcome.astype(jnp.float32)
    backward_slots = (
        jnp.zeros((devices, capacity), jnp.float32).at[home_dev, slot_index].set(-resid)
    )
    returned = lax.all_to_all(backward_slots, "shard", split_axis=0, concat_axis=0, tiled=True)
    dscore = jax.ops.segment_sum(returned.reshape(-1), wanted_rows, num_segments=local_rows)
    dscore = dscore + jax.ops.segment_sum(resid, pair_left, num_segments=local_rows)
    _, pull = jax.vjp(activate, pre)
    dpre32 = pull(dscore[:, None] * w_out.astype(jnp.float32)[None, :])[0]
    dpre = dpre32.astype(jnp.bfloat16)
    grad_bias = jnp.sum(dpre32, axis=0)
    grad_score = jnp.dot(
        dscore, hidden, precision=lax.Precision.HIGHEST, preferred_element_type=jnp.float32
    )
    term_head = jnp.stack([grad_bias, grad_score], axis=1)
    term_weight = lax.dot_general(
        embeddings, dpre, (((0,), (0,)), ((), ())), preferred_element_type=jnp.float32
    )
    return (
        lax.psum_scatter(term_weight, "shard", scatter_dimension=0, tiled=True),
        lax.psum_scatter(term_head, "shard", scatter_dimension=0, tiled=True),
    )


def per_device(embeddings, w_in, bias, w_out, pair_left, pair_home, pair_remote, outcome):
    rows = embeddings.shape[0]
    depth, units = w_in.shape
    n = lax.axis_size("shard")
    small = (
        n & (n - 1) == 0
        and 2 <= n
        and n * rows <= 2048
        and rows % LANES == 0
        and 2 * rows <= 8 * LANES
        and depth % 16 == 0
        and units % (2 * LANES) == 0
        and pair_left.shape[0] % (16 * LANES) == 0
        and pair_left.shape[0] <= 128 * LANES
        and rows <= 256
    )
    if not small:
        return by_collectives(
            embeddings, w_in, bias, w_out, pair_left, pair_home, pair_remote, outcome
        )
    return by_ppermute(
        embeddings, w_in, bias, w_out, pair_left, pair_home, pair_remote, outcome
    )


def solution(mesh):
    in_specs = (
        P("shard", None),
        P("shard", "grp"),
        P("grp"),
        P("grp"),
        P("shard"),
        P("shard", None),
        P("shard"),
        P("shard"),
    )
    out_specs = (P("shard", "grp"), P(("grp", "shard"), None))
    return jax.shard_map(
        per_device, mesh=mesh, in_specs=in_specs, out_specs=out_specs, check_vma=False
    )
```

profile of v0, /device:TPU:9, one launch (start us, length us, event | category | flops | bytes accessed | tf_op | source)
XLA Modules:
  0.0 65.5 jit_solution(5557090699925563653)
XLA Ops:
  0.6 0.7 %collective-permute-start = (bf16[256,1280]{1,0:T(8,128)(2,1)}, bf16[256,1280]{1,0:T(8,128)(2,1)S(1)}, u32[]{:S(2)}, u32[]{:S(2)}) collective-permute-start(bf16[256,1280]{1,0:T(8,128)(2,1)} %own.1), channel_id=1, source_target_pairs={{0,1},{1,0},{2,3},{3,2},{4,5},{5,4},{6,7},{7,6},{8,9},{9,8},{10,11... | collective-permute-start | bytes 1966088 | tf_op jit(solution)/shard_map/ppermute | solution.py:229
  1.4 2.5 %collective-permute-start.4 = (bf16[160,512]{1,0:T(8,128)(2,1)}, bf16[160,512]{1,0:T(8,128)(2,1)S(1)}, u32[]{:S(2)}, u32[]{:S(2)}) collective-permute-start(bf16[160,512]{1,0:T(8,128)(2,1)} %refs_4_.1), channel_id=1, source_target_pairs={{0,4},{1,5},{2,6},{3,7},{4,0},{5,1},{6,2},{7,3},{8,12},{9,13},{10,... | collective-permute-start | bytes 491528 | tf_op jit(solution)/shard_map/ppermute | solution.py:229
  4.0 1.5 %select_convert_fusion.own = s16[8,4,16,128]{3,2,1,0:T(8,128)(2,1)} fusion(s32[16,128]{1,0:T(8,128)} %bitcast.5, s32[16,128]{1,0:T(8,128)} %bitcast.6, s32[16,128]{1,0:T(8,128)} %bitcast.7, s32[16,128]{1,0:T(8,128)} %bitcast.8, pred[4]{0:T(512)(128)(4,1)S(1)} %get-tuple-element.30, pred[4]{0:T(512)(128)(4,1)S(1)} %get-tuple-element.31, ...), kind=kLoop, calls=%fused_computation | loop fusion | flops 262144 | bytes 163852 | tf_op jit(solution)/shard_map/convert_element_type | solution.py:248
  5.5 6.7 %all-to-all-start.1 = ((s16[8,4,16,128]{3,2,1,0:T(8,128)(2,1)}), s16[8,4,16,128]{3,2,1,0:T(8,128)(2,1)S(1)}, u32[]{:S(2)}, u32[]{:S(2)}) async-start(s16[8,4,16,128]{3,2,1,0:T(8,128)(2,1)} %select_convert_fusion.own), calls=%async_computation.1 | async-start | bytes 262144 | tf_op jit(solution)/shard_map/all_to_all | solution.py:249
  12.8 1.8 %collective-permute-done.4.refs_8_ = bf16[160,512]{1,0:T(8,128)(2,1)S(1)} collective-permute-done((bf16[160,512]{1,0:T(8,128)(2,1)}, bf16[160,512]{1,0:T(8,128)(2,1)S(1)}, u32[]{:S(2)}, u32[]{:S(2)}) %collective-permute-start.4) | collective-permute-done | bytes 163872 | tf_op jit(solution)/shard_map/ppermute | solution.py:229
  14.6 3.3 %collective-permute-start.5 = (bf16[160,512]{1,0:T(8,128)(2,1)S(1)}, bf16[160,512]{1,0:T(8,128)(2,1)S(1)}, u32[]{:S(2)}, u32[]{:S(2)}) collective-permute-start(bf16[160,512]{1,0:T(8,128)(2,1)S(1)} %collective-permute-done.4.refs_8_), channel_id=1, source_target_pairs={{0,1},{1,0},{2,3},{3,2},{4,5},{5,4},{6,7},{7,6},{8,9},{9,8},{10,11... | collective-permute-start | bytes 491528 | tf_op jit(solution)/shard_map/ppermute | solution.py:229
  17.9 2.3 %collective-permute-done.6.refs_10_ = bf16[160,512]{1,0:T(8,128)(2,1)S(1)} collective-permute-done((bf16[160,512]{1,0:T(8,128)(2,1)}, bf16[160,512]{1,0:T(8,128)(2,1)S(1)}, u32[]{:S(2)}, u32[]{:S(2)}) %collective-permute-start.6) | collective-permute-done | bytes 163872 | tf_op jit(solution)/shard_map/ppermute | solution.py:229
  20.2 1.9 %collective-permute-start.7 = (bf16[160,512]{1,0:T(8,128)(2,1)S(1)}, bf16[160,512]{1,0:T(8,128)(2,1)S(1)}, u32[]{:S(2)}, u32[]{:S(2)}) collective-permute-start(bf16[160,512]{1,0:T(8,128)(2,1)S(1)} %collective-permute-done.6.refs_10_), channel_id=1, source_target_pairs={{0,1},{1,0},{2,3},{3,2},{4,5},{5,4},{6,7},{7,6},{8,9},{9,8},{10,11... | collective-permute-start | bytes 491528 | tf_op jit(solution)/shard_map/ppermute | solution.py:229
  22.1 0.7 %reshape.19.refs_3_.refs_5_ = bf16[1,512]{1,0:T(2,128)(2,1)S(1)} reshape(bf16[512]{0:T(512)(128)(2,1)} %param.11) | data formatting | bytes 2048 | tf_op jit(solution)/shard_map/reshape | solution.py:260
  22.8 0.7 %reshape.18.refs_2_ = bf16[1,512]{1,0:T(2,128)(2,1)S(1)} reshape(bf16[512]{0:T(512)(128)(2,1)} %param.10) | data formatting | bytes 2048 | tf_op jit(solution)/shard_map/reshape | solution.py:260
  23.5 1.1 %copy-done = bf16[256,1280]{1,0:T(8,128)(2,1)S(1)} copy-done((bf16[256,1280]{1,0:T(8,128)(2,1)S(1)}, bf16[256,1280]{1,0:T(8,128)(2,1)}, u32[]{:S(2)}) %copy-start) | copy-done | bytes 655384
  24.6 0.9 %copy-done.6 = bf16[160,512]{1,0:T(8,128)(2,1)S(1)} copy-done((bf16[160,512]{1,0:T(8,128)(2,1)S(1)}, bf16[160,512]{1,0:T(8,128)(2,1)}, u32[]{:S(2)}) %copy-start.6) | copy-done | bytes 163864
  25.5 2.0 %shard_map.95 = (f32[32,4,128]{2,1,0:T(4,128)}, bf16[512,256]{1,0:T(8,128)(2,1)S(1)}, f32[512,256]{1,0:T(8,128)S(1)}) custom-call(bf16[256,1280]{1,0:T(8,128)(2,1)S(1)} %copy-done, bf16[256,1280]{1,0:T(8,128)(2,1)S(1)} %collective-permute-done.refs_1_.partner, bf16[1,512]{1,0:T(2,128)(2,1)S(1)} %reshape.18.refs_2_, ...), custom_call_target="tpu_custom_call" | custom-call | flops 335544320 | bytes 1048576 | tf_op jit(solution)/shard_map/pallas_call | solution.py:27
  27.5 0.8 %copy-done.2 = f32[512,256]{1,0:T(8,128)} copy-done((f32[512,256]{1,0:T(8,128)}, f32[512,256]{1,0:T(8,128)S(1)}, u32[]{:S(2)}) %copy-start.2) | copy-done | bytes 524312
  28.3 0.7 %copy-done.4 = bf16[512,256]{1,0:T(8,128)(2,1)} copy-done((bf16[512,256]{1,0:T(8,128)(2,1)}, bf16[512,256]{1,0:T(8,128)(2,1)S(1)}, u32[]{:S(2)}) %copy-start.4) | copy-done | bytes 262168
  29.0 0.7 %copy-done.7 = s16[8,4,16,128]{3,2,1,0:T(8,128)(2,1)} copy-done((s16[8,4,16,128]{3,2,1,0:T(8,128)(2,1)}, s16[8,4,16,128]{3,2,1,0:T(8,128)(2,1)S(1)}, u32[]{:S(2)}) %copy-start.7) | copy-done | bytes 131096
  29.7 4.8 %all-to-all-start = ((f32[32,4,128]{2,1,0:T(4,128)}), f32[32,4,128]{2,1,0:T(4,128)}, u32[]{:S(2)}, u32[]{:S(2)}) async-start(f32[32,4,128]{2,1,0:T(4,128)} %get-tuple-element.16), calls=%async_computation | async-start | bytes 131072 | tf_op jit(solution)/shard_map/all_to_all | solution.py:272
  34.5 0.9 %copy-done.8 = s16[8,4,16,128]{3,2,1,0:T(8,128)(2,1)S(1)} copy-done((s16[8,4,16,128]{3,2,1,0:T(8,128)(2,1)S(1)}, s16[8,4,16,128]{3,2,1,0:T(8,128)(2,1)}, u32[]{:S(2)}) %copy-start.8) | copy-done | bytes 131096
  35.4 4.5 %shard_map.96.counts = f32[256,2176]{1,0:T(8,128)S(1)} custom-call(s16[8,4,16,128]{3,2,1,0:T(8,128)(2,1)} %select_convert_fusion.own, s16[8,4,16,128]{3,2,1,0:T(8,128)(2,1)S(1)} %copy-done.8), custom_call_target="tpu_custom_call" | custom-call | flops 4294967296 | bytes 1048576 | tf_op jit(solution)/shard_map/pallas_call | solution.py:27
  39.8 0.7 %all-to-all-done.received = f32[32,4,128]{2,1,0:T(4,128)} async-done(((f32[32,4,128]{2,1,0:T(4,128)}), f32[32,4,128]{2,1,0:T(4,128)}, u32[]{:S(2)}, u32[]{:S(2)}) %all-to-all-start) | async-done | bytes 65568 | tf_op jit(solution)/shard_map/all_to_all | solution.py:272
  40.6 1.4 %shard_map.97.refs_0_ = f32[256,1]{1,0:T(8,128)S(1)} custom-call(f32[32,4,128]{2,1,0:T(4,128)} %all-to-all-done.received, f32[256,2176]{1,0:T(8,128)S(1)} %shard_map.96.counts), custom_call_target="tpu_custom_call" | custom-call | flops 524288 | bytes 1048576 | tf_op jit(solution)/shard_map/pallas_call | solution.py:27
  43.4 0.9 %shard_map.99 = (f32[160,256]{1,0:T(8,128)S(1)}, f32[2,256]{1,0:T(2,128)S(1)}, s16[168,256]{1,0:T(8,128)(2,1)S(1)}, s16[168,256]{1,0:T(8,128)(2,1)S(1)}, s16[168...) custom-call(f32[256,1]{1,0:T(8,128)S(1)} %shard_map.97.refs_0_, ...), custom_call_target="tpu_custom_call" | custom-call | flops 335544320 | bytes 1048576 | tf_op jit(solution)/shard_map/pallas_call | solution.py:27
  44.3 1.4 %collective-permute-start.10 = (s16[168,256]{1,0:T(8,128)(2,1)S(1)}, s16[168,256]{1,0:T(8,128)(2,1)S(1)}, u32[]{:S(2)}, u32[]{:S(2)}) collective-permute-start(s16[168,256]{1,0:T(8,128)(2,1)S(1)} %get-tuple-element.22), channel_id=1, source_target_pairs={{0,2},{1,3},{2,0},{3,1},{4,6},{5,7},{6,4},{7,5},{8,10},{9,11},{10,... | collective-permute-start | bytes 258056 | tf_op jit(solution)/shard_map/ppermute | solution.py:229
  45.7 0.7 %collective-permute-start.11 = (s16[168,256]{1,0:T(8,128)(2,1)S(1)}, s16[168,256]{1,0:T(8,128)(2,1)S(1)}, u32[]{:S(2)}, u32[]{:S(2)}) collective-permute-start(s16[168,256]{1,0:T(8,128)(2,1)S(1)} %get-tuple-element.23), channel_id=1, source_target_pairs={{0,3},{1,2},{2,1},{3,0},{4,7},{5,6},{6,5},{7,4},{8,11},{9,10},{10,... | collective-permute-start | bytes 258056 | tf_op jit(solution)/shard_map/ppermute | solution.py:229
  46.4 1.4 %collective-permute-start.12 = (s16[168,256]{1,0:T(8,128)(2,1)S(1)}, s16[168,256]{1,0:T(8,128)(2,1)S(1)}, u32[]{:S(2)}, u32[]{:S(2)}) collective-permute-start(s16[168,256]{1,0:T(8,128)(2,1)S(1)} %get-tuple-element.24), channel_id=1, source_target_pairs={{0,4},{1,5},{2,6},{3,7},{4,0},{5,1},{6,2},{7,3},{8,12},{9,13},{10,... | collective-permute-start | bytes 258056 | tf_op jit(solution)/shard_map/ppermute | solution.py:229
  47.8 1.0 %collective-permute-start.13 = (s16[168,256]{1,0:T(8,128)(2,1)S(1)}, s16[168,256]{1,0:T(8,128)(2,1)S(1)}, u32[]{:S(2)}, u32[]{:S(2)}) collective-permute-start(s16[168,256]{1,0:T(8,128)(2,1)S(1)} %get-tuple-element.25), channel_id=1, source_target_pairs={{0,5},{1,4},{2,7},{3,6},{4,1},{5,0},{6,3},{7,2},{8,13},{9,12},{10,... | collective-permute-start | bytes 258056 | tf_op jit(solution)/shard_map/ppermute | solution.py:229
  49.3 1.5 %collective-permute-start.15 = (s16[168,256]{1,0:T(8,128)(2,1)S(1)}, s16[168,256]{1,0:T(8,128)(2,1)S(1)}, u32[]{:S(2)}, u32[]{:S(2)}) collective-permute-start(s16[168,256]{1,0:T(8,128)(2,1)S(1)} %get-tuple-element.27), channel_id=1, source_target_pairs={{0,7},{1,6},{2,5},{3,4},{4,3},{5,2},{6,1},{7,0},{8,15},{9,14},{10,... | collective-permute-start | bytes 258056 | tf_op jit(solution)/shard_map/ppermute | solution.py:229
  51.3 1.5 %collective-permute-done.12.refs_5_ = s16[168,256]{1,0:T(8,128)(2,1)S(1)} collective-permute-done((s16[168,256]{1,0:T(8,128)(2,1)S(1)}, s16[168,256]{1,0:T(8,128)(2,1)S(1)}, u32[]{:S(2)}, u32[]{:S(2)}) %collective-permute-start.12) | collective-permute-done | bytes 86048 | tf_op jit(solution)/shard_map/ppermute | solution.py:229
  52.8 6.3 %collective-permute-done.13.refs_6_ = s16[168,256]{1,0:T(8,128)(2,1)S(1)} collective-permute-done((s16[168,256]{1,0:T(8,128)(2,1)S(1)}, s16[168,256]{1,0:T(8,128)(2,1)S(1)}, u32[]{:S(2)}, u32[]{:S(2)}) %collective-permute-start.13) | collective-permute-done | bytes 86048 | tf_op jit(solution)/shard_map/ppermute | solution.py:229
  59.1 3.5 %collective-permute-done.14.refs_7_ = s16[168,256]{1,0:T(8,128)(2,1)S(1)} collective-permute-done((s16[168,256]{1,0:T(8,128)(2,1)S(1)}, s16[168,256]{1,0:T(8,128)(2,1)S(1)}, u32[]{:S(2)}, u32[]{:S(2)}) %collective-permute-start.14) | collective-permute-done | bytes 86048 | tf_op jit(solution)/shard_map/ppermute | solution.py:229
  62.6 1.9 %collective-permute-done.15.refs_8_ = s16[168,256]{1,0:T(8,128)(2,1)S(1)} collective-permute-done((s16[168,256]{1,0:T(8,128)(2,1)S(1)}, s16[168,256]{1,0:T(8,128)(2,1)S(1)}, u32[]{:S(2)}, u32[]{:S(2)}) %collective-permute-start.15) | collective-permute-done | bytes 86048 | tf_op jit(solution)/shard_map/ppermute | solution.py:229
  64.5 0.9 %shard_map.100 = (f32[160,512]{1,0:T(8,128)}, f32[2,64]{1,0:T(2,128)}) custom-call(f32[160,256]{1,0:T(8,128)S(1)} %get-tuple-element.19.refs_0_, f32[2,256]{1,0:T(2,128)S(1)} %get-tuple-element.20.refs_1_, s16[168,256]{1,0:T(8,128)(2,1)S(1)} %collective-permute-done.9.refs_2_, s16[168,256]{1,0:T(8,128)(2,1)S(1)} %collective-permute-done.10.refs_3_, ...), custom_call_target="tpu_custom_call" | custom-call | bytes 1048576 | tf_op jit(solution)/shard_map/pallas_call | solution.py:27
  (33 shorter events, 3.1 us)
Async XLA Ops:
  0.6 22.9 %collective-permute-start = (bf16[256,1280]{1,0:T(8,128)(2,1)}, bf16[256,1280]{1,0:T(8,128)(2,1)S(1)}, u32[]{:S(2)}, u32[]{:S(2)}) collective-permute-start(bf16[256,1280]{1,0:T(8,128)(2,1)} %own.1), channel_id=1, source_target_pairs={{0,1},{1,0},{2,3},{3,2},{4,5},{5,4},{6,7},{7,6},{8,9},{9,8},{10,11... | collective-permute-start | bytes 1966088 | tf_op jit(solution)/shard_map/ppermute | solution.py:229
  1.4 11.3 %collective-permute-start.2 = (bf16[160,512]{1,0:T(8,128)(2,1)}, bf16[160,512]{1,0:T(8,128)(2,1)S(1)}, u32[]{:S(2)}, u32[]{:S(2)}) collective-permute-start(bf16[160,512]{1,0:T(8,128)(2,1)} %refs_4_.1), channel_id=1, source_target_pairs={{0,2},{1,3},{2,0},{3,1},{4,6},{5,7},{6,4},{7,5},{8,10},{9,11},{10,... | collective-permute-start | bytes 491528 | tf_op jit(solution)/shard_map/ppermute | solution.py:229
  1.4 13.2 %collective-permute-start.4 = (bf16[160,512]{1,0:T(8,128)(2,1)}, bf16[160,512]{1,0:T(8,128)(2,1)S(1)}, u32[]{:S(2)}, u32[]{:S(2)}) collective-permute-start(bf16[160,512]{1,0:T(8,128)(2,1)} %refs_4_.1), channel_id=1, source_target_pairs={{0,4},{1,5},{2,6},{3,7},{4,0},{5,1},{6,2},{7,3},{8,12},{9,13},{10,... | collective-permute-start | bytes 491528 | tf_op jit(solution)/shard_map/ppermute | solution.py:229
  3.8 16.4 %collective-permute-start.6 = (bf16[160,512]{1,0:T(8,128)(2,1)}, bf16[160,512]{1,0:T(8,128)(2,1)S(1)}, u32[]{:S(2)}, u32[]{:S(2)}) collective-permute-start(bf16[160,512]{1,0:T(8,128)(2,1)} %refs_4_.1), channel_id=1, source_target_pairs={{0,6},{1,7},{2,4},{3,5},{4,2},{5,3},{6,0},{7,1},{8,14},{9,15},{10,... | collective-permute-start | bytes 491528 | tf_op jit(solution)/shard_map/ppermute | solution.py:229
  5.5 23.5 %all-to-all-start.1 = ((s16[8,4,16,128]{3,2,1,0:T(8,128)(2,1)}), s16[8,4,16,128]{3,2,1,0:T(8,128)(2,1)S(1)}, u32[]{:S(2)}, u32[]{:S(2)}) async-start(s16[8,4,16,128]{3,2,1,0:T(8,128)(2,1)} %select_convert_fusion.own), calls=%async_computation.1 | async-start | bytes 262144 | tf_op jit(solution)/shard_map/all_to_all | solution.py:249
  12.3 11.2 %collective-permute-start.1 = (bf16[160,512]{1,0:T(8,128)(2,1)}, bf16[160,512]{1,0:T(8,128)(2,1)S(1)}, u32[]{:S(2)}, u32[]{:S(2)}) collective-permute-start(bf16[160,512]{1,0:T(8,128)(2,1)} %refs_4_.1), channel_id=1, source_target_pairs={{0,1},{1,0},{2,3},{3,2},{4,5},{5,4},{6,7},{7,6},{8,9},{9,8},{10,11... | collective-permute-start | bytes 491528 | tf_op jit(solution)/shard_map/ppermute | solution.py:229
  12.7 10.8 %collective-permute-start.3 = (bf16[160,512]{1,0:T(8,128)(2,1)S(1)}, bf16[160,512]{1,0:T(8,128)(2,1)S(1)}, u32[]{:S(2)}, u32[]{:S(2)}) collective-permute-start(bf16[160,512]{1,0:T(8,128)(2,1)S(1)} %collective-permute-done.2.refs_6_), channel_id=1, source_target_pairs={{0,1},{1,0},{2,3},{3,2},{4,5},{5,4},{6,7},{7,6},{8,9},{9,8},{10,11... | collective-permute-start | bytes 491528 | tf_op jit(solution)/shard_map/ppermute | solution.py:229
  14.6 8.9 %collective-permute-start.5 = (bf16[160,512]{1,0:T(8,128)(2,1)S(1)}, bf16[160,512]{1,0:T(8,128)(2,1)S(1)}, u32[]{:S(2)}, u32[]{:S(2)}) collective-permute-start(bf16[160,512]{1,0:T(8,128)(2,1)S(1)} %collective-permute-done.4.refs_8_), channel_id=1, source_target_pairs={{0,1},{1,0},{2,3},{3,2},{4,5},{5,4},{6,7},{7,6},{8,9},{9,8},{10,11... | collective-permute-start | bytes 491528 | tf_op jit(solution)/shard_map/ppermute | solution.py:229
  20.2 3.3 %collective-permute-start.7 = (bf16[160,512]{1,0:T(8,128)(2,1)S(1)}, bf16[160,512]{1,0:T(8,128)(2,1)S(1)}, u32[]{:S(2)}, u32[]{:S(2)}) collective-permute-start(bf16[160,512]{1,0:T(8,128)(2,1)S(1)} %collective-permute-done.6.refs_10_), channel_id=1, source_target_pairs={{0,1},{1,0},{2,3},{3,2},{4,5},{5,4},{6,7},{7,6},{8,9},{9,8},{10,11... | collective-permute-start | bytes 491528 | tf_op jit(solution)/shard_map/ppermute | solution.py:229
  23.5 1.1 %copy-start = (bf16[256,1280]{1,0:T(8,128)(2,1)S(1)}, bf16[256,1280]{1,0:T(8,128)(2,1)}, u32[]{:S(2)}) copy-start(bf16[256,1280]{1,0:T(8,128)(2,1)} %own.1) | copy-start | bytes 1966084
  24.6 0.9 %copy-start.6 = (bf16[160,512]{1,0:T(8,128)(2,1)S(1)}, bf16[160,512]{1,0:T(8,128)(2,1)}, u32[]{:S(2)}) copy-start(bf16[160,512]{1,0:T(8,128)(2,1)} %refs_4_.1) | copy-start | bytes 491524
  27.5 0.8 %copy-start.2 = (f32[512,256]{1,0:T(8,128)}, f32[512,256]{1,0:T(8,128)S(1)}, u32[]{:S(2)}) copy-start(f32[512,256]{1,0:T(8,128)S(1)} %get-tuple-element.18.refs_4_) | copy-start | bytes 1572868
  28.3 0.7 %copy-start.4 = (bf16[512,256]{1,0:T(8,128)(2,1)}, bf16[512,256]{1,0:T(8,128)(2,1)S(1)}, u32[]{:S(2)}) copy-start(bf16[512,256]{1,0:T(8,128)(2,1)S(1)} %get-tuple-element.17.refs_3_) | copy-start | bytes 786436
  29.0 0.7 %copy-start.7 = (s16[8,4,16,128]{3,2,1,0:T(8,128)(2,1)}, s16[8,4,16,128]{3,2,1,0:T(8,128)(2,1)S(1)}, u32[]{:S(2)}) copy-start(s16[8,4,16,128]{3,2,1,0:T(8,128)(2,1)S(1)} %all-to-all-done.1.pairs) | copy-start | bytes 393220
  29.7 10.9 %all-to-all-start = ((f32[32,4,128]{2,1,0:T(4,128)}), f32[32,4,128]{2,1,0:T(4,128)}, u32[]{:S(2)}, u32[]{:S(2)}) async-start(f32[32,4,128]{2,1,0:T(4,128)} %get-tuple-element.16), calls=%async_computation | async-start | bytes 131072 | tf_op jit(solution)/shard_map/all_to_all | solution.py:272
  34.5 0.9 %copy-start.8 = (s16[8,4,16,128]{3,2,1,0:T(8,128)(2,1)S(1)}, s16[8,4,16,128]{3,2,1,0:T(8,128)(2,1)}, u32[]{:S(2)}) copy-start(s16[8,4,16,128]{3,2,1,0:T(8,128)(2,1)} %copy-done.7) | copy-start | bytes 393220
  39.8 2.6 %copy-start.1 = (bf16[256,1280]{1,0:T(8,128)(2,1)S(1)}, bf16[256,1280]{1,0:T(8,128)(2,1)}, u32[]{:S(2)}) copy-start(bf16[256,1280]{1,0:T(8,128)(2,1)} %own.1) | copy-start | bytes 1966084
  40.6 2.8 %copy-start.3 = (f32[512,256]{1,0:T(8,128)S(1)}, f32[512,256]{1,0:T(8,128)}, u32[]{:S(2)}) copy-start(f32[512,256]{1,0:T(8,128)} %copy-done.2) | copy-start | bytes 1572868
  40.6 2.8 %copy-start.5 = (bf16[512,256]{1,0:T(8,128)(2,1)S(1)}, bf16[512,256]{1,0:T(8,128)(2,1)}, u32[]{:S(2)}) copy-start(bf16[512,256]{1,0:T(8,128)(2,1)} %copy-done.4) | copy-start | bytes 786436
  42.0 1.4 %collective-permute-start.8 = (f32[256,1]{1,0:T(8,128)S(1)}, f32[256,1]{1,0:T(8,128)S(1)}, u32[]{:S(2)}, u32[]{:S(2)}) collective-permute-start(f32[256,1]{1,0:T(8,128)S(1)} %shard_map.97.refs_0_), channel_id=1, source_target_pairs={{0,1},{1,0},{2,3},{3,2},{4,5},{5,4},{6,7},{7,6},{8,9},{9,8},{10,11... | collective-permute-start | bytes 3080 | tf_op jit(solution)/shard_map/ppermute | solution.py:229
  44.3 5.0 %collective-permute-start.10 = (s16[168,256]{1,0:T(8,128)(2,1)S(1)}, s16[168,256]{1,0:T(8,128)(2,1)S(1)}, u32[]{:S(2)}, u32[]{:S(2)}) collective-permute-start(s16[168,256]{1,0:T(8,128)(2,1)S(1)} %get-tuple-element.22), channel_id=1, source_target_pairs={{0,2},{1,3},{2,0},{3,1},{4,6},{5,7},{6,4},{7,5},{8,10},{9,11},{10,... | collective-permute-start | bytes 258056 | tf_op jit(solution)/shard_map/ppermute | solution.py:229
  45.7 5.1 %collective-permute-start.11 = (s16[168,256]{1,0:T(8,128)(2,1)S(1)}, s16[168,256]{1,0:T(8,128)(2,1)S(1)}, u32[]{:S(2)}, u32[]{:S(2)}) collective-permute-start(s16[168,256]{1,0:T(8,128)(2,1)S(1)} %get-tuple-element.23), channel_id=1, source_target_pairs={{0,3},{1,2},{2,1},{3,0},{4,7},{5,6},{6,5},{7,4},{8,11},{9,10},{10,... | collective-permute-start | bytes 258056 | tf_op jit(solution)/shard_map/ppermute | solution.py:229
  46.4 6.4 %collective-permute-start.12 = (s16[168,256]{1,0:T(8,128)(2,1)S(1)}, s16[168,256]{1,0:T(8,128)(2,1)S(1)}, u32[]{:S(2)}, u32[]{:S(2)}) collective-permute-start(s16[168,256]{1,0:T(8,128)(2,1)S(1)} %get-tuple-element.24), channel_id=1, source_target_pairs={{0,4},{1,5},{2,6},{3,7},{4,0},{5,1},{6,2},{7,3},{8,12},{9,13},{10,... | collective-permute-start | bytes 258056 | tf_op jit(solution)/shard_map/ppermute | solution.py:229
  47.8 11.3 %collective-permute-start.13 = (s16[168,256]{1,0:T(8,128)(2,1)S(1)}, s16[168,256]{1,0:T(8,128)(2,1)S(1)}, u32[]{:S(2)}, u32[]{:S(2)}) collective-permute-start(s16[168,256]{1,0:T(8,128)(2,1)S(1)} %get-tuple-element.25), channel_id=1, source_target_pairs={{0,5},{1,4},{2,7},{3,6},{4,1},{5,0},{6,3},{7,2},{8,13},{9,12},{10,... | collective-permute-start | bytes 258056 | tf_op jit(solution)/shard_map/ppermute | solution.py:229
  48.8 13.8 %collective-permute-start.14 = (s16[168,256]{1,0:T(8,128)(2,1)S(1)}, s16[168,256]{1,0:T(8,128)(2,1)S(1)}, u32[]{:S(2)}, u32[]{:S(2)}) collective-permute-start(s16[168,256]{1,0:T(8,128)(2,1)S(1)} %get-tuple-element.26), channel_id=1, source_target_pairs={{0,6},{1,7},{2,4},{3,5},{4,2},{5,3},{6,0},{7,1},{8,14},{9,15},{10,... | collective-permute-start | bytes 258056 | tf_op jit(solution)/shard_map/ppermute | solution.py:229
  49.3 15.2 %collective-permute-start.15 = (s16[168,256]{1,0:T(8,128)(2,1)S(1)}, s16[168,256]{1,0:T(8,128)(2,1)S(1)}, u32[]{:S(2)}, u32[]{:S(2)}) collective-permute-start(s16[168,256]{1,0:T(8,128)(2,1)S(1)} %get-tuple-element.27), channel_id=1, source_target_pairs={{0,7},{1,6},{2,5},{3,4},{4,3},{5,2},{6,1},{7,0},{8,15},{9,14},{10,... | collective-permute-start | bytes 258056 | tf_op jit(solution)/shard_map/ppermute | solution.py:229
  50.8 13.8 %collective-permute-start.9 = (s16[168,256]{1,0:T(8,128)(2,1)S(1)}, s16[168,256]{1,0:T(8,128)(2,1)S(1)}, u32[]{:S(2)}, u32[]{:S(2)}) collective-permute-start(s16[168,256]{1,0:T(8,128)(2,1)S(1)} %get-tuple-element.21), channel_id=1, source_target_pairs={{0,1},{1,0},{2,3},{3,2},{4,5},{5,4},{6,7},{7,6},{8,9},{9,8},{10,11... | collective-permute-start | bytes 258056 | tf_op jit(solution)/shard_map/ppermute | solution.py:229
where the time goes:
time: 65.9 us; the launch traced here: 65.5 us
  starting transfers between devices  28 us (42%)
  waiting for transfers between devices  18.7 us (28%)
  Pallas kernels  10.1 us (15%)
  local copies, waits for them, and re-layouts  6.44 us (10%)
  other arithmetic  1.51 us (2%)
  between operations  0.74 us (1%)
    ppermute x16, waiting for transfers between devices, swap(): return lax.ppermute(value, 'shard', [(i, i ^ m) for i in range(n)])  18 us
    ppermute x16, starting transfers between devices, swap(): return lax.ppermute(value, 'shard', [(i, i ^ m) for i in range(n)])  16.5 us
    pallas_call x6, Pallas kernels, call(): pl.pallas_call(body, out_shape=outputs, in_specs=[pl.BlockSpec(memory_spa...  10.1 us
    all_to_all x1, starting transfers between devices, by_ppermute(): lists = lax.all_to_all(pairs, 'shard', 0, 0, tiled=True)  6.75 us
    unnamed x18, local copies, waits for them, and re-layouts  5.08 us
    all_to_all x1, starting transfers between devices, by_ppermute(): received = lax.all_to_all(score, ('grp', 'shard'), 0, 0, tiled=True)  4.75 us
    convert_element_type x1, other arithmetic, by_ppermute(): pairs = pairs.astype(jnp.int16)  1.5 us
    reshape x2, local copies, waits for them, and re-layouts, by_ppermute(): bias, w_out = (bias.reshape(1, -1), w_out.reshape(1, -1))  1.36 us
  transfers between devices with their start and end apart: 18, of which 8 were waited for; matrix products, arithmetic and copies ran while one was open for 4% of the time, Pallas kernels for 10%

commit v1 on v0

--- a/solution.py
+++ b/solution.py
@@ -35,8 +35,8 @@
     )(*inputs)
 
 
-def pair_rows(ref, owner, part, chunk):
-    return ref[owner, part, pl.ds(chunk, 1), :].astype(jnp.int32)
+def pair_rows(ref, part, chunk):
+    return ref[part, pl.ds(chunk, 1), :].astype(jnp.int32)
 
 
 def transpose_kernel(own, partner, out):
@@ -47,37 +47,40 @@
         out[:, pl.ds(at, rows)] = ref[...].T
 
 
-def count_kernel(own, pairs, out, lefts):
+def count_kernel(*refs):
+    lists, (out, lefts) = refs[:-2], refs[-2:]
+    own = lists[0]
     shard = lax.axis_index("shard")
     rows = out.shape[0]
-    owners, _, chunks, _ = pairs.shape
+    chunks = own.shape[1]
     ids = lax.broadcasted_iota(jnp.int32, (rows, LANES), 0).astype(BF16)
     nought = jnp.zeros((), BF16)
 
-    def table(ref, owner, home=None, sums=False):
+    def table(ref, home=None, sums=False):
         columns, added = [], jnp.zeros((rows, LANES), BF16)
         for q in range(chunks):
-            row = pair_rows(ref, owner, 0, q)
+            row = pair_rows(ref, 0, q)
             if home is not None:
-                row = jnp.where(pair_rows(ref, owner, 1, q) == home, pair_rows(ref, owner, 2, q), -1)
+                row = jnp.where(pair_rows(ref, 1, q) == home, pair_rows(ref, 2, q), -1)
             hit = ids == row.astype(BF16)
             columns.append(jnp.where(hit, jnp.ones((), BF16), nought).astype(jnp.float8_e5m2))
             if sums:
-                half = jnp.where(pair_rows(ref, owner, 3, q) == 1, -0.5, 0.5).astype(BF16)
+                half = jnp.where(pair_rows(ref, 3, q) == 1, -0.5, 0.5).astype(BF16)
                 added = added + jnp.where(hit, half, nought)
         return jnp.concatenate(columns, axis=1), added.astype(F32)
 
-    lefts[...], total = table(own, 0, sums=True)
-    for o in range(owners):
-        here, _ = table(own, 0, home=o)
-        there, added = table(pairs, o, home=shard, sums=True)
-        theirs, _ = table(pairs, o)
+    lefts[...], total = table(own, sums=True)
+    for m, ref in enumerate(lists):
+        owner = shard ^ m
+        here, _ = table(own, home=owner)
+        there, added = table(ref, home=shard, sums=True)
+        theirs, _ = table(ref)
         total = total - added
-        out[:, o * rows : (o + 1) * rows] = 0.5 * (
+        out[:, pl.ds(pl.multiple_of(owner * rows, rows), rows)] = 0.5 * (
             lax.dot_general(lefts[...], here, NT, preferred_element_type=F32)
             + lax.dot_general(there, theirs, NT, preferred_element_type=F32)
         )
-    out[:, owners * rows :] = total
+    out[:, len(lists) * rows :] = total
 
 
 def forward_kernel(*refs):
@@ -159,61 +162,99 @@
         dscore[span, :] = jnp.sum(total, axis=1, keepdims=True)
 
 
-def gradient_kernel(*refs):
-    near, next_to, flipped, hidden, slope, w_out = refs[:6]
-    kept, heads = refs[6:8]
-    messages = refs[8:-2]
-    terms, sent = refs[-2:]
+def dpre_of(dscores, rows_at, hidden, slope, weights, sent):
+    half = hidden.shape[1]
+    bias_sum, score_sum = jnp.zeros((1, half), F32), jnp.zeros((1, half), F32)
+    for r in range(dscores.shape[0] // LANES):
+        span = slice(r * LANES, (r + 1) * LANES)
+        there = pl.ds(pl.multiple_of(rows_at + r * LANES, LANES), LANES)
+        dscore = dscores[span, :]
+        dpre = (dscore * weights) * slope[there, :]
+        bias_sum = bias_sum + jnp.sum(dpre, axis=0, keepdims=True)
+        score_sum = score_sum + jnp.sum(dscore * hidden[there, :].astype(F32), axis=0, keepdims=True)
+        sent[span, :] = dpre.astype(BF16)
+    return jnp.concatenate([bias_sum, score_sum], axis=0)
+
+
+def weights_of(w_out, half):
+    core = lax.axis_index("shard") % 2
+    return w_out[:, pl.ds(pl.multiple_of(core * half, half), half)].astype(F32)
+
+
+def own_kernel(dscores, flipped, hidden, slope, w_out, terms, sums, sent):
+    core = lax.axis_index("shard") % 2
+    rows = dscores.shape[0]
+    at = pl.multiple_of(core * rows, rows)
+    sums[...] = dpre_of(dscores, at, hidden, slope, weights_of(w_out, hidden.shape[1]), sent)
+    terms[...] = jnp.dot(flipped[:, pl.ds(at, rows)], sent[...], preferred_element_type=F32)
+
+
+def block_of(m, flipped, own_terms, sent, depth):
     shard = lax.axis_index("shard")
-    core = shard % 2
-    rows = near.shape[0]
-    half = hidden.shape[1]
-    depth = kept.shape[0]
-    lane = pl.multiple_of(core * half, half)
-    weights = w_out[:, pl.ds(lane, half)].astype(F32)
-    bias_sum = jnp.zeros((1, half), F32)
-    score_sum = jnp.zeros((1, half), F32)
-    for j, ref in enumerate((near, next_to)):
-        for r in range(rows // LANES):
-            there = pl.ds(pl.multiple_of((core ^ j) * rows + r * LANES, LANES), LANES)
-            dscore = ref[r * LANES : (r + 1) * LANES, :]
-            dpre = (dscore * weights) * slope[there, :]
-            bias_sum = bias_sum + jnp.sum(dpre, axis=0, keepdims=True)
-            score_sum = score_sum + jnp.sum(dscore * hidden[there, :].astype(F32), axis=0, keepdims=True)
-            sent[there, :] = dpre.astype(BF16)
-    terms[...] = jnp.dot(flipped[...], sent[...], preferred_element_type=F32)
-    kept[...] = terms[pl.ds(pl.multiple_of(shard * depth, depth), depth), :]
-    heads[...] = jnp.concatenate([bias_sum, score_sum], axis=0)
-    extra = coded(bias_sum) + coded(score_sum)
+    rows = sent.shape[0]
+    at = pl.ds(pl.multiple_of((shard ^ m) * depth, depth), depth)
+    columns = pl.ds(pl.multiple_of((1 - shard % 2) * rows, rows), rows)
+    return own_terms[at, :] + jnp.dot(flipped[at, columns], sent[...], preferred_element_type=F32)
+
+
+def write_message(ref, block, heads):
+    depth, half = block.shape
+    extra = coded(heads[0:1, :]) + coded(heads[1:2, :])
+    power = exponent_of(jnp.max(jnp.abs(block), axis=0, keepdims=True), 32000.0)
+    ref[:depth, :] = jnp.round(block * jnp.exp2(-power)).astype(jnp.int32).astype(jnp.int16)
+    pad = jnp.zeros((TAIL - 1 - len(extra), half), F32)
+    tail = jnp.concatenate([power] + extra + [pad], axis=0)
+    ref[depth:, :] = tail.astype(jnp.int32).astype(jnp.int16)
+
+
+def far_kernel(first, dscores, own_terms, own_sums, flipped, hidden, slope, w_out, heads, sent, *messages):
+    core = lax.axis_index("shard") % 2
+    at = (1 - core) * dscores.shape[0]
+    sums = dpre_of(dscores, at, hidden, slope, weights_of(w_out, hidden.shape[1]), sent)
+    heads[...] = own_sums[...] + sums
+    for m, ref in enumerate(messages, first):
+        write_message(ref, block_of(m, flipped, own_terms, sent, ref.shape[0] - TAIL), heads[...])
+
+
+def near_kernel(heads, sent, own_terms, flipped, kept, *messages):
+    kept[...] = block_of(0, flipped, own_terms, sent, kept.shape[0])
     for m, ref in enumerate(messages, 1):
-        block = terms[pl.ds(pl.multiple_of((shard ^ m) * depth, depth), depth), :]
-        power = exponent_of(jnp.max(jnp.abs(block), axis=0, keepdims=True), 32000.0)
-        ref[:depth, :] = jnp.round(block * jnp.exp2(-power)).astype(jnp.int32).astype(jnp.int16)
-        pad = jnp.zeros((TAIL - 1 - len(extra), half), F32)
-        tail = jnp.concatenate([power] + extra + [pad], axis=0)
-        ref[depth:, :] = tail.astype(jnp.int32).astype(jnp.int16)
-
-
-def sum_kernel(*refs):
-    kept, heads = refs[:2]
-    messages = refs[2:-2]
-    weight, head = refs[-2:]
-    shard = lax.axis_index("shard")
-    core = shard % 2
-    depth, half = kept.shape
-    sums = [kept[...], jnp.zeros_like(kept)]
-    tops = [heads[...], jnp.zeros_like(heads)]
-    for m, ref in enumerate(messages, 1):
+        write_message(ref, block_of(m, flipped, own_terms, sent, kept.shape[0]), heads[...])
+
+
+def added(first, sums, tops, messages):
+    for m, ref in enumerate(messages, first):
+        depth = ref.shape[0] - TAIL
         tail = ref[depth:, :].astype(jnp.int32).astype(F32)
         sums[m % 2] = sums[m % 2] + ref[:depth, :].astype(jnp.int32).astype(F32) * jnp.exp2(tail[0:1, :])
         tops[m % 2] = tops[m % 2] + jnp.concatenate([decoded(tail, 1), decoded(tail, 4)], axis=0)
+
+
+def first_sum_kernel(kept, heads, *refs):
+    messages, (sums_out, tops_out) = refs[:-2], refs[-2:]
+    sums = [kept[...], jnp.zeros_like(kept)]
+    tops = [heads[...], jnp.zeros_like(heads)]
+    added(1, sums, tops, messages)
+    for k in range(2):
+        sums_out[k] = sums[k]
+        tops_out[k] = tops[k]
+
+
+def last_sum_kernel(first, sums_in, tops_in, *refs):
+    messages, (weight, head) = refs[:-2], refs[-2:]
+    shard = lax.axis_index("shard")
+    core = shard % 2
+    half = sums_in.shape[2]
+    sums = [sums_in[k] for k in range(2)]
+    tops = [tops_in[k] for k in range(2)]
+    added(first, sums, tops, messages)
     weight[:, pl.ds(pl.multiple_of(core * half, half), half)] = sums[0]
     weight[:, pl.ds(pl.multiple_of((1 - core) * half, half), half)] = sums[1]
     units = head.shape[1]
-    first = shard * units
-    chosen = jnp.where(first // half == core, tops[0], tops[1])
+    start = shard * units
+    chosen = jnp.where(start // half == core, tops[0], tops[1])
     chosen = jnp.concatenate([chosen, jnp.zeros((6, half), F32)], axis=0)
-    head[...] = pltpu.roll(chosen, (half - first % half) % half, 1)[:2, :units]
+    head[...] = pltpu.roll(chosen, (half - start % half) % half, 1)[:2, :units]
 
 
 def by_ppermute(embeddings, w_in, bias, w_out, pair_left, pair_home, pair_remote, outcome):
@@ -239,20 +280,20 @@
         return [got[m] for m in range(n)]
 
     blocks = spread(w_in)
-    tile = (1, 1, chunks, LANES)
+    tile = (1, chunks, LANES)
     columns = [a.reshape(tile) for a in (pair_left, pair_home, pair_remote, outcome)]
-    part = lax.broadcasted_iota(jnp.int32, (n, 4, chunks, LANES), 1)
+    part = lax.broadcasted_iota(jnp.int32, (4, chunks, LANES), 0)
     pairs = columns[3]
     for k in (2, 1, 0):
         pairs = jnp.where(part == k, columns[k], pairs)
     pairs = pairs.astype(jnp.int16)
-    lists = lax.all_to_all(pairs, "shard", 0, 0, tiled=True)
+    lists = spread(pairs)
     partner = swap(embeddings, 1)
     shape = jax.ShapeDtypeStruct
     (flipped,) = call(transpose_kernel, (embeddings, partner), [shape((channels, 2 * rows), BF16)])
     (counts,) = call(
         count_kernel,
-        (pairs, lists),
+        lists,
         [shape((rows, n * rows + LANES), F32)],
         [pltpu.VMEM((rows, pair_count), jnp.float8_e5m2)],
         flops=4 * rows * n * rows * pair_count,
@@ -275,18 +316,36 @@
     )
     next_to = swap(near, 1)
     message = shape((depth + TAIL, half), jnp.int16)
-    kept, heads, *messages = call(
-        gradient_kernel,
-        (near, next_to, flipped, hidden, slope, w_out),
-        [shape((depth, half), F32), shape((2, half), F32)] + [message] * (n - 1),
-        [pltpu.VMEM((channels, half), F32), pltpu.VMEM((2 * rows, half), BF16)],
-        flops=4 * rows * channels * half,
-    )
-    order = sorted(range(1, n), key=lambda m: -(m // 2))
-    got = {m: swap(messages[m - 1], m) for m in order}
+    first = n // 2
+    own_terms, own_sums = call(
+        own_kernel,
+        (near, flipped, hidden, slope, w_out),
+        [shape((channels, half), F32), shape((2, half), F32)],
+        [pltpu.VMEM((rows, half), BF16)],
+        flops=2 * rows * channels * half,
+    )
+    heads, sent, *distant = call(
+        functools.partial(far_kernel, first),
+        (next_to, own_terms, own_sums, flipped, hidden, slope, w_out),
+        [shape((2, half), F32), shape((rows, half), BF16)] + [message] * (n - first),
+        flops=rows * channels * half,
+    )
+    kept, *close = call(
+        near_kernel,
+        (heads, sent, own_terms, flipped),
+        [shape((depth, half), F32)] + [message] * (first - 1),
+        flops=rows * channels * half,
+    )
+    messages = dict(enumerate(close + distant, 1))
+    got = {m: swap(messages[m], m) for m in range(n - 1, 0, -1)}
+    sums, tops = call(
+        first_sum_kernel,
+        (kept, heads, *[got[m] for m in range(1, first)]),
+        [shape((2, depth, half), F32), shape((2, 2, half), F32)],
+    )
     weight, head = call(
-        sum_kernel,
-        (kept, heads, *[got[m] for m in range(1, n)]),
+        functools.partial(last_sum_kernel, first),
+        (sums, tops, *[got[m] for m in range(first, n)]),
         [shape((depth, hidden_units), F32), shape((2, hidden_units // n), F32)],
     )
     return weight, head.T
@@ -345,7 +404,7 @@
     n = lax.axis_size("shard")
     small = (
         n & (n - 1) == 0
-        and 2 <= n
+        and 4 <= n
         and n * rows <= 2048
         and rows % LANES == 0
         and 2 * rows <= 8 * LANES

time: 65.9 us -> 70.6 us (1.071)
  waiting for transfers between devices: 18.7 us -> 26.9 us
  Pallas kernels: 10.1 us -> 8.53 us
  starting transfers between devices: 28 us -> 26.8 us
    ppermute x16 -> x23, waiting for transfers between devices: 18 us -> 26.3 us  [swap(): return lax.ppermute(value, 'shard', [(i, i ^ m) for i in range(n)])]
    all_to_all x1 -> x0, starting transfers between devices: 6.75 us -> none  [by_ppermute(): lists = lax.all_to_all(pairs, 'shard', 0, 0, tiled=True)]
    all_to_all x1, starting transfers between devices: 4.75 us -> 8.24 us  [by_ppermute(): received = lax.all_to_all(score, ('grp', 'shard'), 0, 0, tiled=True)]
    ppermute x16 -> x23, starting transfers between devices: 16.5 us -> 18.5 us  [swap(): return lax.ppermute(value, 'shard', [(i, i ^ m) for i in range(n)])]
    pallas_call x6 -> x9, Pallas kernels: 10.1 us -> 8.53 us  [call(): pl.pallas_call(body, out_shape=outputs, in_specs=[pl.BlockSpec(memory_spa...]
    unnamed x18 -> x10, local copies, waits for them, and re-layouts: 5.08 us -> 5.03 us
  transfers between devices with their start and end apart: 18 -> 24, of which waited for: 8 -> 10; matrix products, arithmetic and copies ran while one was open for 4% -> 3% of each run, Pallas kernels for 10% -> 9%
where the time goes in v1:
time: 70.6 us; the launch traced here: 70.3 us
  waiting for transfers between devices  26.9 us (38%)
  starting transfers between devices  26.8 us (38%)
  Pallas kernels  8.53 us (12%)
  local copies, waits for them, and re-layouts  6.39 us (9%)
  other arithmetic  0.84 us (1%)
  between operations  0.76 us (1%)
    ppermute x23, waiting for transfers between devices, swap(): return lax.ppermute(value, 'shard', [(i, i ^ m) for i in range(n)])  26.3 us
    ppermute x23, starting transfers between devices, swap(): return lax.ppermute(value, 'shard', [(i, i ^ m) for i in range(n)])  18.5 us
    pallas_call x9, Pallas kernels, call(): pl.pallas_call(body, out_shape=outputs, in_specs=[pl.BlockSpec(memory_spa...  8.53 us
    all_to_all x1, starting transfers between devices, by_ppermute(): received = lax.all_to_all(score, ('grp', 'shard'), 0, 0, tiled=True)  8.24 us
    unnamed x10, local copies, waits for them, and re-layouts  5.03 us
  transfers between devices with their start and end apart: 24, of which 10 were waited for; matrix products, arithmetic and copies ran while one was open for 3% of the time, Pallas kernels for 9%

profile of v1, /device:TPU:9, one launch (start us, length us, event | category | flops | bytes accessed | tf_op | source)
XLA Modules:
  0.0 70.3 jit_solution(12618435127937891071)
XLA Ops:
  0.7 2.5 %collective-permute-start.4 = (bf16[160,512]{1,0:T(8,128)(2,1)}, bf16[160,512]{1,0:T(8,128)(2,1)S(1)}, u32[]{:S(2)}, u32[]{:S(2)}) collective-permute-start(bf16[160,512]{1,0:T(8,128)(2,1)} %refs_4_.1), channel_id=1, source_target_pairs={{0,4},{1,5},{2,6},{3,7},{4,0},{5,1},{6,2},{7,3},{8,12},{9,13},{10,... | collective-permute-start | bytes 491528 | tf_op jit(solution)/shard_map/ppermute | solution.py:270
  3.3 1.5 %collective-permute-start = (bf16[256,1280]{1,0:T(8,128)(2,1)}, bf16[256,1280]{1,0:T(8,128)(2,1)S(1)}, u32[]{:S(2)}, u32[]{:S(2)}) collective-permute-start(bf16[256,1280]{1,0:T(8,128)(2,1)} %own.1), channel_id=1, source_target_pairs={{0,1},{1,0},{2,3},{3,2},{4,5},{5,4},{6,7},{7,6},{8,9},{9,8},{10,11... | collective-permute-start | bytes 1966088 | tf_op jit(solution)/shard_map/ppermute | solution.py:270
  4.9 0.8 %select_convert_fusion.refs_0_ = s16[4,16,128]{2,1,0:T(8,128)(2,1)S(1)} fusion(s32[16,128]{1,0:T(8,128)} %bitcast.5, s32[16,128]{1,0:T(8,128)} %bitcast.6, s32[16,128]{1,0:T(8,128)} %bitcast.7, s32[16,128]{1,0:T(8,128)} %bitcast.8, pred[4]{0:T(512)(128)(4,1)S(1)} %get-tuple-element.40, pred[4]{0:T(512)(128)(4,1)S(1)} %get-tuple-element.41, ...), kind=kLoop, calls=%fused_computation | loop fusion | flops 32768 | bytes 49164 | tf_op jit(solution)/shard_map/convert_element_type | solution.py:289
  5.7 0.9 %collective-permute-start.9 = (s16[4,16,128]{2,1,0:T(8,128)(2,1)S(1)}, s16[4,16,128]{2,1,0:T(8,128)(2,1)S(1)}, u32[]{:S(2)}, u32[]{:S(2)}) collective-permute-start(s16[4,16,128]{2,1,0:T(8,128)(2,1)S(1)} %select_convert_fusion.refs_0_), channel_id=1, source_target_pairs={{0,2},{1,3},{2,0},{3,1},{4,6},{5,7},{6,4},{7,5},{8,10},{9,11},{10,... | collective-permute-start | bytes 49160 | tf_op jit(solution)/shard_map/ppermute | solution.py:270
  6.6 6.5 %collective-permute-done.9.refs_2_ = s16[4,16,128]{2,1,0:T(8,128)(2,1)S(1)} collective-permute-done((s16[4,16,128]{2,1,0:T(8,128)(2,1)S(1)}, s16[4,16,128]{2,1,0:T(8,128)(2,1)S(1)}, u32[]{:S(2)}, u32[]{:S(2)}) %collective-permute-start.9) | collective-permute-done | bytes 16416 | tf_op jit(solution)/shard_map/ppermute | solution.py:270
  13.1 0.6 collective-permute-start.11
  13.7 3.6 %collective-permute-done.11.refs_4_ = s16[4,16,128]{2,1,0:T(8,128)(2,1)S(1)} collective-permute-done((s16[4,16,128]{2,1,0:T(8,128)(2,1)S(1)}, s16[4,16,128]{2,1,0:T(8,128)(2,1)S(1)}, u32[]{:S(2)}, u32[]{:S(2)}) %collective-permute-start.11) | collective-permute-done | bytes 16416 | tf_op jit(solution)/shard_map/ppermute | solution.py:270
  17.3 0.7 collective-permute-start.13
  18.0 1.9 %collective-permute-done.13.refs_6_ = s16[4,16,128]{2,1,0:T(8,128)(2,1)S(1)} collective-permute-done((s16[4,16,128]{2,1,0:T(8,128)(2,1)S(1)}, s16[4,16,128]{2,1,0:T(8,128)(2,1)S(1)}, u32[]{:S(2)}, u32[]{:S(2)}) %collective-permute-start.13) | collective-permute-done | bytes 16416 | tf_op jit(solution)/shard_map/ppermute | solution.py:270
  19.9 3.5 %collective-permute-start.1 = (bf16[160,512]{1,0:T(8,128)(2,1)}, bf16[160,512]{1,0:T(8,128)(2,1)S(1)}, u32[]{:S(2)}, u32[]{:S(2)}) collective-permute-start(bf16[160,512]{1,0:T(8,128)(2,1)} %refs_4_.1), channel_id=1, source_target_pairs={{0,1},{1,0},{2,3},{3,2},{4,5},{5,4},{6,7},{7,6},{8,9},{9,8},{10,11... | collective-permute-start | bytes 491528 | tf_op jit(solution)/shard_map/ppermute | solution.py:270
  23.4 0.5 collective-permute-start.5
  24.0 0.7 reshape.18.refs_2_
  24.7 0.7 reshape.19.refs_3_.w_out
  26.4 1.1 %copy-done = bf16[256,1280]{1,0:T(8,128)(2,1)S(1)} copy-done((bf16[256,1280]{1,0:T(8,128)(2,1)S(1)}, bf16[256,1280]{1,0:T(8,128)(2,1)}, u32[]{:S(2)}) %copy-start) | copy-done | bytes 655384
  27.5 0.9 %copy-done.4 = bf16[160,512]{1,0:T(8,128)(2,1)S(1)} copy-done((bf16[160,512]{1,0:T(8,128)(2,1)S(1)}, bf16[160,512]{1,0:T(8,128)(2,1)}, u32[]{:S(2)}) %copy-start.4) | copy-done | bytes 163864
  28.4 2.0 %shard_map.95 = (f32[32,4,128]{2,1,0:T(4,128)}, bf16[512,256]{1,0:T(8,128)(2,1)S(1)}, f32[512,256]{1,0:T(8,128)S(1)}) custom-call(bf16[256,1280]{1,0:T(8,128)(2,1)S(1)} %copy-done, bf16[256,1280]{1,0:T(8,128)(2,1)S(1)} %collective-permute-done.refs_1_.partner, bf16[1,512]{1,0:T(2,128)(2,1)S(1)} %reshape.18.refs_2_, ...), custom_call_target="tpu_custom_call" | custom-call | flops 335544320 | bytes 1048576 | tf_op jit(solution)/shard_map/pallas_call | solution.py:27
  30.4 8.2 %all-to-all-start = ((f32[32,4,128]{2,1,0:T(4,128)}), f32[32,4,128]{2,1,0:T(4,128)S(1)}, u32[]{:S(2)}, u32[]{:S(2)}) async-start(f32[32,4,128]{2,1,0:T(4,128)} %get-tuple-element.21), calls=%async_computation | async-start | bytes 131072 | tf_op jit(solution)/shard_map/all_to_all | solution.py:313
  38.7 3.6 %shard_map.96.counts = f32[256,2176]{1,0:T(8,128)S(1)} custom-call(s16[4,16,128]{2,1,0:T(8,128)(2,1)S(1)} %select_convert_fusion.refs_0_, s16[4,16,128]{2,1,0:T(8,128)(2,1)S(1)} %collective-permute-done.8.refs_1_, s16[4,16,128]{2,1,0:T(8,128)(2,1)S(1)} %collective-permute-done.9.refs_2_, s16[4,16,128]{2,1,0:T(8,128)(2,1)S(1)} %collective-permute-done.10.refs_3_, ...), custom_call_target="tpu_custom_call" | custom-call | flops 4294967296 | bytes 1048576 | tf_op jit(solution)/shard_map/pallas_call | solution.py:27
  42.3 1.4 %copy-done.2 = f32[256,2176]{1,0:T(8,128)} copy-done((f32[256,2176]{1,0:T(8,128)}, f32[256,2176]{1,0:T(8,128)S(1)}, u32[]{:S(2)}) %copy-start.2) | copy-done | bytes 2228248
  44.1 0.7 all-to-all-done.received
  44.8 1.6 %copy-done.3 = f32[256,2176]{1,0:T(8,128)S(1)} copy-done((f32[256,2176]{1,0:T(8,128)S(1)}, f32[256,2176]{1,0:T(8,128)}, u32[]{:S(2)}) %copy-start.3) | copy-done | bytes 2228248
  47.7 0.6 collective-permute-done.15.dscores
  49.5 1.3 %collective-permute-start.17 = (s16[168,256]{1,0:T(8,128)(2,1)S(1)}, s16[168,256]{1,0:T(8,128)(2,1)S(1)}, u32[]{:S(2)}, u32[]{:S(2)}) collective-permute-start(s16[168,256]{1,0:T(8,128)(2,1)S(1)} %get-tuple-element.30), channel_id=1, source_target_pairs={{0,2},{1,3},{2,0},{3,1},{4,6},{5,7},{6,4},{7,5},{8,10},{9,11},{10,... | collective-permute-start | bytes 258056 | tf_op jit(solution)/shard_map/ppermute | solution.py:270
  51.2 1.5 %collective-permute-start.19 = (s16[168,256]{1,0:T(8,128)(2,1)S(1)}, s16[168,256]{1,0:T(8,128)(2,1)S(1)}, u32[]{:S(2)}, u32[]{:S(2)}) collective-permute-start(s16[168,256]{1,0:T(8,128)(2,1)S(1)} %get-tuple-element.34), channel_id=1, source_target_pairs={{0,4},{1,5},{2,6},{3,7},{4,0},{5,1},{6,2},{7,3},{8,12},{9,13},{10,... | collective-permute-start | bytes 258056 | tf_op jit(solution)/shard_map/ppermute | solution.py:270
  52.7 1.1 %collective-permute-start.20 = (s16[168,256]{1,0:T(8,128)(2,1)S(1)}, s16[168,256]{1,0:T(8,128)(2,1)S(1)}, u32[]{:S(2)}, u32[]{:S(2)}) collective-permute-start(s16[168,256]{1,0:T(8,128)(2,1)S(1)} %get-tuple-element.35), channel_id=1, source_target_pairs={{0,5},{1,4},{2,7},{3,6},{4,1},{5,0},{6,3},{7,2},{8,13},{9,12},{10,... | collective-permute-start | bytes 258056 | tf_op jit(solution)/shard_map/ppermute | solution.py:270
  53.9 0.5 collective-permute-start.21
  54.4 1.2 %collective-permute-start.22 = (s16[168,256]{1,0:T(8,128)(2,1)S(1)}, s16[168,256]{1,0:T(8,128)(2,1)S(1)}, u32[]{:S(2)}, u32[]{:S(2)}) collective-permute-start(s16[168,256]{1,0:T(8,128)(2,1)S(1)} %get-tuple-element.37), channel_id=1, source_target_pairs={{0,7},{1,6},{2,5},{3,4},{4,3},{5,2},{6,1},{7,0},{8,15},{9,14},{10,... | collective-permute-start | bytes 258056 | tf_op jit(solution)/shard_map/ppermute | solution.py:270
  55.9 1.8 %collective-permute-done.19.refs_0_ = s16[168,256]{1,0:T(8,128)(2,1)S(1)} collective-permute-done((s16[168,256]{1,0:T(8,128)(2,1)S(1)}, s16[168,256]{1,0:T(8,128)(2,1)S(1)}, u32[]{:S(2)}, u32[]{:S(2)}) %collective-permute-start.19) | collective-permute-done | bytes 86048 | tf_op jit(solution)/shard_map/ppermute | solution.py:270
  57.7 6.1 %collective-permute-done.20.refs_1_ = s16[168,256]{1,0:T(8,128)(2,1)S(1)} collective-permute-done((s16[168,256]{1,0:T(8,128)(2,1)S(1)}, s16[168,256]{1,0:T(8,128)(2,1)S(1)}, u32[]{:S(2)}, u32[]{:S(2)}) %collective-permute-start.20) | collective-permute-done | bytes 86048 | tf_op jit(solution)/shard_map/ppermute | solution.py:270
  63.8 3.5 %collective-permute-done.21.refs_2_ = s16[168,256]{1,0:T(8,128)(2,1)S(1)} collective-permute-done((s16[168,256]{1,0:T(8,128)(2,1)S(1)}, s16[168,256]{1,0:T(8,128)(2,1)S(1)}, u32[]{:S(2)}, u32[]{:S(2)}) %collective-permute-start.21) | collective-permute-done | bytes 86048 | tf_op jit(solution)/shard_map/ppermute | solution.py:270
  67.3 2.1 %collective-permute-done.22.refs_3_ = s16[168,256]{1,0:T(8,128)(2,1)S(1)} collective-permute-done((s16[168,256]{1,0:T(8,128)(2,1)S(1)}, s16[168,256]{1,0:T(8,128)(2,1)S(1)}, u32[]{:S(2)}, u32[]{:S(2)}) %collective-permute-start.22) | collective-permute-done | bytes 86048 | tf_op jit(solution)/shard_map/ppermute | solution.py:270
  69.4 0.8 %shard_map.103 = (f32[160,512]{1,0:T(8,128)}, f32[2,64]{1,0:T(2,128)}) custom-call(f32[2,160,256]{2,1,0:T(8,128)S(1)} %get-tuple-element.32.sums_in, f32[2,2,256]{2,1,0:T(2,128)S(1)} %get-tuple-element.33.tops_in, s16[168,256]{1,0:T(8,128)(2,1)S(1)} %collective-permute-done.19.refs_0_, s16[168,256]{1,0:T(8,128)(2,1)S(1)} %collective-permute-done.20.refs_1_, ...), custom_call_target="tpu_custom_call" | custom-call | bytes 1048576 | tf_op jit(solution)/shard_map/pallas_call | solution.py:27
  (40 shorter events, 5.0 us)
Async XLA Ops:
  0.6 22.8 %collective-permute-start.2 = (bf16[160,512]{1,0:T(8,128)(2,1)}, bf16[160,512]{1,0:T(8,128)(2,1)S(1)}, u32[]{:S(2)}, u32[]{:S(2)}) collective-permute-start(bf16[160,512]{1,0:T(8,128)(2,1)} %refs_4_.1), channel_id=1, source_target_pairs={{0,2},{1,3},{2,0},{3,1},{4,6},{5,7},{6,4},{7,5},{8,10},{9,11},{10,... | collective-permute-start | bytes 491528 | tf_op jit(solution)/shard_map/ppermute | solution.py:270
  0.7 22.7 %collective-permute-start.4 = (bf16[160,512]{1,0:T(8,128)(2,1)}, bf16[160,512]{1,0:T(8,128)(2,1)S(1)}, u32[]{:S(2)}, u32[]{:S(2)}) collective-permute-start(bf16[160,512]{1,0:T(8,128)(2,1)} %refs_4_.1), channel_id=1, source_target_pairs={{0,4},{1,5},{2,6},{3,7},{4,0},{5,1},{6,2},{7,3},{8,12},{9,13},{10,... | collective-permute-start | bytes 491528 | tf_op jit(solution)/shard_map/ppermute | solution.py:270
  3.2 20.8 %collective-permute-start.6 = (bf16[160,512]{1,0:T(8,128)(2,1)}, bf16[160,512]{1,0:T(8,128)(2,1)S(1)}, u32[]{:S(2)}, u32[]{:S(2)}) collective-permute-start(bf16[160,512]{1,0:T(8,128)(2,1)} %refs_4_.1), channel_id=1, source_target_pairs={{0,6},{1,7},{2,4},{3,5},{4,2},{5,3},{6,0},{7,1},{8,14},{9,15},{10,... | collective-permute-start | bytes 491528 | tf_op jit(solution)/shard_map/ppermute | solution.py:270
  3.3 23.1 %collective-permute-start = (bf16[256,1280]{1,0:T(8,128)(2,1)}, bf16[256,1280]{1,0:T(8,128)(2,1)S(1)}, u32[]{:S(2)}, u32[]{:S(2)}) collective-permute-start(bf16[256,1280]{1,0:T(8,128)(2,1)} %own.1), channel_id=1, source_target_pairs={{0,1},{1,0},{2,3},{3,2},{4,5},{5,4},{6,7},{7,6},{8,9},{9,8},{10,11... | collective-permute-start | bytes 1966088 | tf_op jit(solution)/shard_map/ppermute | solution.py:270
  5.7 7.4 %collective-permute-start.9 = (s16[4,16,128]{2,1,0:T(8,128)(2,1)S(1)}, s16[4,16,128]{2,1,0:T(8,128)(2,1)S(1)}, u32[]{:S(2)}, u32[]{:S(2)}) collective-permute-start(s16[4,16,128]{2,1,0:T(8,128)(2,1)S(1)} %select_convert_fusion.refs_0_), channel_id=1, source_target_pairs={{0,2},{1,3},{2,0},{3,1},{4,6},{5,7},{6,4},{7,5},{8,10},{9,11},{10,... | collective-permute-start | bytes 49160 | tf_op jit(solution)/shard_map/ppermute | solution.py:270
  13.1 4.2 %collective-permute-start.11 = (s16[4,16,128]{2,1,0:T(8,128)(2,1)S(1)}, s16[4,16,128]{2,1,0:T(8,128)(2,1)S(1)}, u32[]{:S(2)}, u32[]{:S(2)}) collective-permute-start(s16[4,16,128]{2,1,0:T(8,128)(2,1)S(1)} %select_convert_fusion.refs_0_), channel_id=1, source_target_pairs={{0,4},{1,5},{2,6},{3,7},{4,0},{5,1},{6,2},{7,3},{8,12},{9,13},{10,... | collective-permute-start | bytes 49160 | tf_op jit(solution)/shard_map/ppermute | solution.py:270
  17.3 2.6 %collective-permute-start.13 = (s16[4,16,128]{2,1,0:T(8,128)(2,1)S(1)}, s16[4,16,128]{2,1,0:T(8,128)(2,1)S(1)}, u32[]{:S(2)}, u32[]{:S(2)}) collective-permute-start(s16[4,16,128]{2,1,0:T(8,128)(2,1)S(1)} %select_convert_fusion.refs_0_), channel_id=1, source_target_pairs={{0,6},{1,7},{2,4},{3,5},{4,2},{5,3},{6,0},{7,1},{8,14},{9,15},{10,... | collective-permute-start | bytes 49160 | tf_op jit(solution)/shard_map/ppermute | solution.py:270
  19.9 5.5 %collective-permute-start.1 = (bf16[160,512]{1,0:T(8,128)(2,1)}, bf16[160,512]{1,0:T(8,128)(2,1)S(1)}, u32[]{:S(2)}, u32[]{:S(2)}) collective-permute-start(bf16[160,512]{1,0:T(8,128)(2,1)} %refs_4_.1), channel_id=1, source_target_pairs={{0,1},{1,0},{2,3},{3,2},{4,5},{5,4},{6,7},{7,6},{8,9},{9,8},{10,11... | collective-permute-start | bytes 491528 | tf_op jit(solution)/shard_map/ppermute | solution.py:270
  23.4 2.4 %collective-permute-start.3 = (bf16[160,512]{1,0:T(8,128)(2,1)S(1)}, bf16[160,512]{1,0:T(8,128)(2,1)S(1)}, u32[]{:S(2)}, u32[]{:S(2)}) collective-permute-start(bf16[160,512]{1,0:T(8,128)(2,1)S(1)} %collective-permute-done.2.refs_6_), channel_id=1, source_target_pairs={{0,1},{1,0},{2,3},{3,2},{4,5},{5,4},{6,7},{7,6},{8,9},{9,8},{10,11... | collective-permute-start | bytes 491528 | tf_op jit(solution)/shard_map/ppermute | solution.py:270
  23.4 2.5 %collective-permute-start.5 = (bf16[160,512]{1,0:T(8,128)(2,1)S(1)}, bf16[160,512]{1,0:T(8,128)(2,1)S(1)}, u32[]{:S(2)}, u32[]{:S(2)}) collective-permute-start(bf16[160,512]{1,0:T(8,128)(2,1)S(1)} %collective-permute-done.4.refs_8_), channel_id=1, source_target_pairs={{0,1},{1,0},{2,3},{3,2},{4,5},{5,4},{6,7},{7,6},{8,9},{9,8},{10,11... | collective-permute-start | bytes 491528 | tf_op jit(solution)/shard_map/ppermute | solution.py:270
  23.9 2.4 %collective-permute-start.7 = (bf16[160,512]{1,0:T(8,128)(2,1)S(1)}, bf16[160,512]{1,0:T(8,128)(2,1)S(1)}, u32[]{:S(2)}, u32[]{:S(2)}) collective-permute-start(bf16[160,512]{1,0:T(8,128)(2,1)S(1)} %collective-permute-done.6.refs_10_), channel_id=1, source_target_pairs={{0,1},{1,0},{2,3},{3,2},{4,5},{5,4},{6,7},{7,6},{8,9},{9,8},{10,11... | collective-permute-start | bytes 491528 | tf_op jit(solution)/shard_map/ppermute | solution.py:270
  25.4 13.3 %collective-permute-start.8 = (s16[4,16,128]{2,1,0:T(8,128)(2,1)S(1)}, s16[4,16,128]{2,1,0:T(8,128)(2,1)S(1)}, u32[]{:S(2)}, u32[]{:S(2)}) collective-permute-start(s16[4,16,128]{2,1,0:T(8,128)(2,1)S(1)} %select_convert_fusion.refs_0_), channel_id=1, source_target_pairs={{0,1},{1,0},{2,3},{3,2},{4,5},{5,4},{6,7},{7,6},{8,9},{9,8},{10,11... | collective-permute-start | bytes 49160 | tf_op jit(solution)/shard_map/ppermute | solution.py:270
  25.8 12.9 %collective-permute-start.10 = (s16[4,16,128]{2,1,0:T(8,128)(2,1)S(1)}, s16[4,16,128]{2,1,0:T(8,128)(2,1)S(1)}, u32[]{:S(2)}, u32[]{:S(2)}) collective-permute-start(s16[4,16,128]{2,1,0:T(8,128)(2,1)S(1)} %collective-permute-done.9.refs_2_), channel_id=1, source_target_pairs={{0,1},{1,0},{2,3},{3,2},{4,5},{5,4},{6,7},{7,6},{8,9},{9,8},{10,11... | collective-permute-start | bytes 49160 | tf_op jit(solution)/shard_map/ppermute | solution.py:270
  25.9 12.8 %collective-permute-start.12 = (s16[4,16,128]{2,1,0:T(8,128)(2,1)S(1)}, s16[4,16,128]{2,1,0:T(8,128)(2,1)S(1)}, u32[]{:S(2)}, u32[]{:S(2)}) collective-permute-start(s16[4,16,128]{2,1,0:T(8,128)(2,1)S(1)} %collective-permute-done.11.refs_4_), channel_id=1, source_target_pairs={{0,1},{1,0},{2,3},{3,2},{4,5},{5,4},{6,7},{7,6},{8,9},{9,8},{10,11... | collective-permute-start | bytes 49160 | tf_op jit(solution)/shard_map/ppermute | solution.py:270
  26.3 12.4 %collective-permute-start.14 = (s16[4,16,128]{2,1,0:T(8,128)(2,1)S(1)}, s16[4,16,128]{2,1,0:T(8,128)(2,1)S(1)}, u32[]{:S(2)}, u32[]{:S(2)}) collective-permute-start(s16[4,16,128]{2,1,0:T(8,128)(2,1)S(1)} %collective-permute-done.13.refs_6_), channel_id=1, source_target_pairs={{0,1},{1,0},{2,3},{3,2},{4,5},{5,4},{6,7},{7,6},{8,9},{9,8},{10,11... | collective-permute-start | bytes 49160 | tf_op jit(solution)/shard_map/ppermute | solution.py:270
  26.4 1.1 %copy-start = (bf16[256,1280]{1,0:T(8,128)(2,1)S(1)}, bf16[256,1280]{1,0:T(8,128)(2,1)}, u32[]{:S(2)}) copy-start(bf16[256,1280]{1,0:T(8,128)(2,1)} %own.1) | copy-start | bytes 1966084
  27.5 0.9 %copy-start.4 = (bf16[160,512]{1,0:T(8,128)(2,1)S(1)}, bf16[160,512]{1,0:T(8,128)(2,1)}, u32[]{:S(2)}) copy-start(bf16[160,512]{1,0:T(8,128)(2,1)} %refs_4_.1) | copy-start | bytes 491524
  30.4 14.3 %all-to-all-start = ((f32[32,4,128]{2,1,0:T(4,128)}), f32[32,4,128]{2,1,0:T(4,128)S(1)}, u32[]{:S(2)}, u32[]{:S(2)}) async-start(f32[32,4,128]{2,1,0:T(4,128)} %get-tuple-element.21), calls=%async_computation | async-start | bytes 131072 | tf_op jit(solution)/shard_map/all_to_all | solution.py:313
  38.7 5.0 %copy-start.1 = (bf16[256,1280]{1,0:T(8,128)(2,1)S(1)}, bf16[256,1280]{1,0:T(8,128)(2,1)}, u32[]{:S(2)}) copy-start(bf16[256,1280]{1,0:T(8,128)(2,1)} %own.1) | copy-start | bytes 1966084
  42.3 1.4 %copy-start.2 = (f32[256,2176]{1,0:T(8,128)}, f32[256,2176]{1,0:T(8,128)S(1)}, u32[]{:S(2)}) copy-start(f32[256,2176]{1,0:T(8,128)S(1)} %shard_map.96.counts) | copy-start | bytes 6684676
  44.7 1.6 %copy-start.3 = (f32[256,2176]{1,0:T(8,128)S(1)}, f32[256,2176]{1,0:T(8,128)}, u32[]{:S(2)}) copy-start(f32[256,2176]{1,0:T(8,128)} %copy-done.2) | copy-start | bytes 6684676
  46.9 1.4 %collective-permute-start.15 = (f32[256,1]{1,0:T(8,128)S(1)}, f32[256,1]{1,0:T(8,128)S(1)}, u32[]{:S(2)}, u32[]{:S(2)}) collective-permute-start(f32[256,1]{1,0:T(8,128)S(1)} %shard_map.97.dscores), channel_id=1, source_target_pairs={{0,1},{1,0},{2,3},{3,2},{4,5},{5,4},{6,7},{7,6},{8,9},{9,8},{10,11... | collective-permute-start | bytes 3080 | tf_op jit(solution)/shard_map/ppermute | solution.py:270
  49.0 4.8 %collective-permute-start.16 = (s16[168,256]{1,0:T(8,128)(2,1)S(1)}, s16[168,256]{1,0:T(8,128)(2,1)S(1)}, u32[]{:S(2)}, u32[]{:S(2)}) collective-permute-start(s16[168,256]{1,0:T(8,128)(2,1)S(1)} %get-tuple-element.29), channel_id=1, source_target_pairs={{0,1},{1,0},{2,3},{3,2},{4,5},{5,4},{6,7},{7,6},{8,9},{9,8},{10,11... | collective-permute-start | bytes 258056 | tf_op jit(solution)/shard_map/ppermute | solution.py:270
  49.5 4.9 %collective-permute-start.17 = (s16[168,256]{1,0:T(8,128)(2,1)S(1)}, s16[168,256]{1,0:T(8,128)(2,1)S(1)}, u32[]{:S(2)}, u32[]{:S(2)}) collective-permute-start(s16[168,256]{1,0:T(8,128)(2,1)S(1)} %get-tuple-element.30), channel_id=1, source_target_pairs={{0,2},{1,3},{2,0},{3,1},{4,6},{5,7},{6,4},{7,5},{8,10},{9,11},{10,... | collective-permute-start | bytes 258056 | tf_op jit(solution)/shard_map/ppermute | solution.py:270
  50.8 5.0 %collective-permute-start.18 = (s16[168,256]{1,0:T(8,128)(2,1)S(1)}, s16[168,256]{1,0:T(8,128)(2,1)S(1)}, u32[]{:S(2)}, u32[]{:S(2)}) collective-permute-start(s16[168,256]{1,0:T(8,128)(2,1)S(1)} %get-tuple-element.31), channel_id=1, source_target_pairs={{0,3},{1,2},{2,1},{3,0},{4,7},{5,6},{6,5},{7,4},{8,11},{9,10},{10,... | collective-permute-start | bytes 258056 | tf_op jit(solution)/shard_map/ppermute | solution.py:270
  51.2 6.5 %collective-permute-start.19 = (s16[168,256]{1,0:T(8,128)(2,1)S(1)}, s16[168,256]{1,0:T(8,128)(2,1)S(1)}, u32[]{:S(2)}, u32[]{:S(2)}) collective-permute-start(s16[168,256]{1,0:T(8,128)(2,1)S(1)} %get-tuple-element.34), channel_id=1, source_target_pairs={{0,4},{1,5},{2,6},{3,7},{4,0},{5,1},{6,2},{7,3},{8,12},{9,13},{10,... | collective-permute-start | bytes 258056 | tf_op jit(solution)/shard_map/ppermute | solution.py:270
  52.7 11.1 %collective-permute-start.20 = (s16[168,256]{1,0:T(8,128)(2,1)S(1)}, s16[168,256]{1,0:T(8,128)(2,1)S(1)}, u32[]{:S(2)}, u32[]{:S(2)}) collective-permute-start(s16[168,256]{1,0:T(8,128)(2,1)S(1)} %get-tuple-element.35), channel_id=1, source_target_pairs={{0,5},{1,4},{2,7},{3,6},{4,1},{5,0},{6,3},{7,2},{8,13},{9,12},{10,... | collective-permute-start | bytes 258056 | tf_op jit(solution)/shard_map/ppermute | solution.py:270
  53.9 13.5 %collective-permute-start.21 = (s16[168,256]{1,0:T(8,128)(2,1)S(1)}, s16[168,256]{1,0:T(8,128)(2,1)S(1)}, u32[]{:S(2)}, u32[]{:S(2)}) collective-permute-start(s16[168,256]{1,0:T(8,128)(2,1)S(1)} %get-tuple-element.36), channel_id=1, source_target_pairs={{0,6},{1,7},{2,4},{3,5},{4,2},{5,3},{6,0},{7,1},{8,14},{9,15},{10,... | collective-permute-start | bytes 258056 | tf_op jit(solution)/shard_map/ppermute | solution.py:270
  54.4 15.0 %collective-permute-start.22 = (s16[168,256]{1,0:T(8,128)(2,1)S(1)}, s16[168,256]{1,0:T(8,128)(2,1)S(1)}, u32[]{:S(2)}, u32[]{:S(2)}) collective-permute-start(s16[168,256]{1,0:T(8,128)(2,1)S(1)} %get-tuple-element.37), channel_id=1, source_target_pairs={{0,7},{1,6},{2,5},{3,4},{4,3},{5,2},{6,1},{7,0},{8,15},{9,14},{10,... | collective-permute-start | bytes 258056 | tf_op jit(solution)/shard_map/ppermute | solution.py:270

commit v2 on v1

--- a/solution.py
+++ b/solution.py
@@ -83,24 +83,48 @@
     out[:, len(lists) * rows :] = total
 
 
-def forward_kernel(*refs):
-    own, partner, bias, w_out = refs[:4]
-    score, hidden, slope, gathered = refs[-4:]
-    blocks = refs[4:-4]
+def late_window(depth):
+    return -(-(2 * depth + LANES // 2) // LANES) * LANES
+
+
+def begin_kernel(late, own, partner, *refs):
+    blocks, (out, gathered) = refs[:-2], refs[-2:]
     shard = lax.axis_index("shard")
     core = shard % 2
     rows = own.shape[0]
     depth = blocks[0].shape[0]
+    half = out.shape[1]
+    lane = pl.multiple_of(core * half, half)
+    n = len(blocks) + 2
+    for m, ref in zip((m for m in range(n) if m not in (late, late + 1)), blocks):
+        gathered[pl.ds(pl.multiple_of((shard ^ m) * depth, depth), depth), :] = ref[:, pl.ds(lane, half)]
+    chip = (shard ^ late) // 2
+    gathered[pl.ds(pl.multiple_of(chip * 2 * depth, 2 * depth), 2 * depth), :] = jnp.zeros((2 * depth, half), BF16)
+    for j, ref in enumerate((own, partner)):
+        at = pl.multiple_of((core ^ j) * rows, rows)
+        out[pl.ds(at, rows), :] = jnp.dot(ref[...], gathered[...], preferred_element_type=F32)
+
+
+def forward_kernel(late, own, partner, bias, w_out, begun, same, other, score, hidden, slope, gathered):
+    shard = lax.axis_index("shard")
+    core = shard % 2
+    rows = own.shape[0]
+    depth = same.shape[0]
     half = hidden.shape[1]
     lane = pl.multiple_of(core * half, half)
-    for m, ref in enumerate(blocks):
-        at = pl.multiple_of((shard ^ m) * depth, depth)
+    window = gathered.shape[0]
+    first = (shard ^ late) // 2 * (2 * depth)
+    tile = pl.multiple_of(first // LANES * LANES, LANES)
+    gathered[...] = jnp.zeros_like(gathered)
+    for k, ref in ((core, same), (1 - core, other)):
+        at = pl.multiple_of(first % LANES + k * depth, 16)
         gathered[pl.ds(at, depth), :] = ref[:, pl.ds(lane, half)]
     shift = bias[:, pl.ds(lane, half)].astype(F32)
     weights = w_out[:, pl.ds(lane, half)]
     for j, ref in enumerate((own, partner)):
         at = pl.multiple_of((core ^ j) * rows, rows)
-        pre = jnp.dot(ref[...], gathered[...], preferred_element_type=F32) + shift
+        late_part = jnp.dot(ref[:, pl.ds(tile, window)], gathered[...], preferred_element_type=F32)
+        pre = (begun[pl.ds(at, rows), :] + late_part) + shift
         square = pre * pre
         scale = 0.7978845608028654
         t = jnp.tanh(scale * (pre + 0.044715 * (square * pre)))
@@ -299,16 +323,24 @@
         flops=4 * rows * n * rows * pair_count,
     )
     bias, w_out = bias.reshape(1, -1), w_out.reshape(1, -1)
+    late = n // 2
+    (begun,) = call(
+        functools.partial(begin_kernel, late),
+        (embeddings, partner, *[blocks[m] for m in range(n) if m not in (late, late + 1)]),
+        [shape((2 * rows, half), F32)],
+        [pltpu.VMEM((channels, half), BF16)],
+        flops=3 * rows * channels * half,
+    )
     score, hidden, slope = call(
-        forward_kernel,
-        (embeddings, partner, bias, w_out, *blocks),
+        functools.partial(forward_kernel, late),
+        (embeddings, partner, bias, w_out, begun, blocks[late], blocks[late + 1]),
         [
             shape((groups * n, 2 * rows // LANES, LANES), F32),
             shape((2 * rows, half), BF16),
             shape((2 * rows, half), F32),
         ],
-        [pltpu.VMEM((channels, half), BF16)],
-        flops=4 * rows * channels * half,
+        [pltpu.VMEM((late_window(depth), half), BF16)],
+        flops=rows * channels * half,
     )
     received = lax.all_to_all(score, ("grp", "shard"), 0, 0, tiled=True)
     (near,) = call(
@@ -410,6 +442,9 @@
         and 2 * rows <= 8 * LANES
         and depth % 16 == 0
         and units % (2 * LANES) == 0
+        and 2 * depth % (LANES // 2) == 0
+        and embeddings.shape[1] == n * depth
+        and (n - 2) * depth // LANES * LANES + late_window(depth) <= n * depth
         and pair_left.shape[0] % (16 * LANES) == 0
         and pair_left.shape[0] <= 128 * LANES
         and rows <= 256

time: 70.6 us -> 70.7 us (level)
    pallas_call x9 -> x10, Pallas kernels: 8.53 us -> 8.71 us  [call(): pl.pallas_call(body, out_shape=outputs, in_specs=[pl.BlockSpec(memory_spa...]
where the time goes in v2:
time: 70.7 us; the launch traced here: 70.3 us
  waiting for transfers between devices  27.1 us (38%)
  starting transfers between devices  26.6 us (38%)
  Pallas kernels  8.71 us (12%)
  local copies, waits for them, and re-layouts  6.39 us (9%)
  other arithmetic  0.84 us (1%)
  between operations  0.79 us (1%)
    ppermute x23, waiting for transfers between devices, swap(): return lax.ppermute(value, 'shard', [(i, i ^ m) for i in range(n)])  26.4 us
    ppermute x23, starting transfers between devices, swap(): return lax.ppermute(value, 'shard', [(i, i ^ m) for i in range(n)])  18.5 us
    pallas_call x10, Pallas kernels, call(): pl.pallas_call(body, out_shape=outputs, in_specs=[pl.BlockSpec(memory_spa...  8.71 us
    all_to_all x1, starting transfers between devices, by_ppermute(): received = lax.all_to_all(score, ('grp', 'shard'), 0, 0, tiled=True)  8.09 us
    unnamed x10, local copies, waits for them, and re-layouts  5.02 us
  transfers between devices with their start and end apart: 24, of which 10 were waited for; matrix products, arithmetic and copies ran while one was open for 3% of the time, Pallas kernels for 9%

profile of v2, /device:TPU:9, one launch (start us, length us, event | category | flops | bytes accessed | tf_op | source)
XLA Modules:
  0.0 70.3 jit_solution(4171480619697828411)
XLA Ops:
  0.7 2.6 %collective-permute-start.4 = (bf16[160,512]{1,0:T(8,128)(2,1)}, bf16[160,512]{1,0:T(8,128)(2,1)S(1)}, u32[]{:S(2)}, u32[]{:S(2)}) collective-permute-start(bf16[160,512]{1,0:T(8,128)(2,1)} %refs_0_.1), channel_id=1, source_target_pairs={{0,6},{1,7},{2,4},{3,5},{4,2},{5,3},{6,0},{7,1},{8,14},{9,15},{10,... | collective-permute-start | bytes 491528 | tf_op jit(solution)/shard_map/ppermute | solution.py:294
  3.3 1.0 %collective-permute-start.6 = (bf16[160,512]{1,0:T(8,128)(2,1)}, bf16[160,512]{1,0:T(8,128)(2,1)S(1)}, u32[]{:S(2)}, u32[]{:S(2)}) collective-permute-start(bf16[160,512]{1,0:T(8,128)(2,1)} %refs_0_.1), channel_id=1, source_target_pairs={{0,4},{1,5},{2,6},{3,7},{4,0},{5,1},{6,2},{7,3},{8,12},{9,13},{10,... | collective-permute-start | bytes 491528 | tf_op jit(solution)/shard_map/ppermute | solution.py:294
  4.2 1.5 %collective-permute-start = (bf16[256,1280]{1,0:T(8,128)(2,1)}, bf16[256,1280]{1,0:T(8,128)(2,1)S(1)}, u32[]{:S(2)}, u32[]{:S(2)}) collective-permute-start(bf16[256,1280]{1,0:T(8,128)(2,1)} %own.5), channel_id=1, source_target_pairs={{0,1},{1,0},{2,3},{3,2},{4,5},{5,4},{6,7},{7,6},{8,9},{9,8},{10,11... | collective-permute-start | bytes 1966088 | tf_op jit(solution)/shard_map/ppermute | solution.py:294
  5.8 0.8 %select_convert_fusion.refs_0_ = s16[4,16,128]{2,1,0:T(8,128)(2,1)S(1)} fusion(s32[16,128]{1,0:T(8,128)} %bitcast.5, s32[16,128]{1,0:T(8,128)} %bitcast.6, s32[16,128]{1,0:T(8,128)} %bitcast.7, s32[16,128]{1,0:T(8,128)} %bitcast.8, pred[4]{0:T(512)(128)(4,1)S(1)} %get-tuple-element.40, pred[4]{0:T(512)(128)(4,1)S(1)} %get-tuple-element.41, ...), kind=kLoop, calls=%fused_computation | loop fusion | flops 32768 | bytes 49164 | tf_op jit(solution)/shard_map/convert_element_type | solution.py:313
  6.7 6.7 %collective-permute-done.9.refs_2_ = s16[4,16,128]{2,1,0:T(8,128)(2,1)S(1)} collective-permute-done((s16[4,16,128]{2,1,0:T(8,128)(2,1)S(1)}, s16[4,16,128]{2,1,0:T(8,128)(2,1)S(1)}, u32[]{:S(2)}, u32[]{:S(2)}) %collective-permute-start.9) | collective-permute-done | bytes 16416 | tf_op jit(solution)/shard_map/ppermute | solution.py:294
  13.7 3.7 %collective-permute-done.11.refs_4_ = s16[4,16,128]{2,1,0:T(8,128)(2,1)S(1)} collective-permute-done((s16[4,16,128]{2,1,0:T(8,128)(2,1)S(1)}, s16[4,16,128]{2,1,0:T(8,128)(2,1)S(1)}, u32[]{:S(2)}, u32[]{:S(2)}) %collective-permute-start.11) | collective-permute-done | bytes 16416 | tf_op jit(solution)/shard_map/ppermute | solution.py:294
  17.4 0.9 %collective-permute-start.13 = (s16[4,16,128]{2,1,0:T(8,128)(2,1)S(1)}, s16[4,16,128]{2,1,0:T(8,128)(2,1)S(1)}, u32[]{:S(2)}, u32[]{:S(2)}) collective-permute-start(s16[4,16,128]{2,1,0:T(8,128)(2,1)S(1)} %select_convert_fusion.refs_0_), channel_id=1, source_target_pairs={{0,6},{1,7},{2,4},{3,5},{4,2},{5,3},{6,0},{7,1},{8,14},{9,15},{10,... | collective-permute-start | bytes 49160 | tf_op jit(solution)/shard_map/ppermute | solution.py:294
  18.3 1.7 %collective-permute-done.13.refs_6_ = s16[4,16,128]{2,1,0:T(8,128)(2,1)S(1)} collective-permute-done((s16[4,16,128]{2,1,0:T(8,128)(2,1)S(1)}, s16[4,16,128]{2,1,0:T(8,128)(2,1)S(1)}, u32[]{:S(2)}, u32[]{:S(2)}) %collective-permute-start.13) | collective-permute-done | bytes 16416 | tf_op jit(solution)/shard_map/ppermute | solution.py:294
  20.0 3.5 %collective-permute-start.1 = (bf16[160,512]{1,0:T(8,128)(2,1)}, bf16[160,512]{1,0:T(8,128)(2,1)S(1)}, u32[]{:S(2)}, u32[]{:S(2)}) collective-permute-start(bf16[160,512]{1,0:T(8,128)(2,1)} %refs_0_.1), channel_id=1, source_target_pairs={{0,1},{1,0},{2,3},{3,2},{4,5},{5,4},{6,7},{7,6},{8,9},{9,8},{10,11... | collective-permute-start | bytes 491528 | tf_op jit(solution)/shard_map/ppermute | solution.py:294
  23.5 0.5 collective-permute-start.5
  24.1 0.7 reshape.18.bias
  24.7 0.7 reshape.19.w_out
  26.5 1.1 %copy-done = bf16[256,1280]{1,0:T(8,128)(2,1)S(1)} copy-done((bf16[256,1280]{1,0:T(8,128)(2,1)S(1)}, bf16[256,1280]{1,0:T(8,128)(2,1)}, u32[]{:S(2)}) %copy-start) | copy-done | bytes 655384
  27.6 0.9 %copy-done.4 = bf16[160,512]{1,0:T(8,128)(2,1)S(1)} copy-done((bf16[160,512]{1,0:T(8,128)(2,1)S(1)}, bf16[160,512]{1,0:T(8,128)(2,1)}, u32[]{:S(2)}) %copy-start.4) | copy-done | bytes 163864
  28.5 0.6 shard_map.95.begun
  29.0 1.6 %shard_map.96 = (f32[32,4,128]{2,1,0:T(4,128)}, bf16[512,256]{1,0:T(8,128)(2,1)S(1)}, f32[512,256]{1,0:T(8,128)S(1)}) custom-call(bf16[256,1280]{1,0:T(8,128)(2,1)S(1)} %copy-done, bf16[256,1280]{1,0:T(8,128)(2,1)S(1)} %collective-permute-done.partner, bf16[1,512]{1,0:T(2,128)(2,1)S(1)} %reshape.18.bias, bf16[1,512]{1,0:T(2,128)(2,1)S(1)} %reshape.19.w_out, ...), custom_call_target="tpu_custom_call" | custom-call | flops 83886080 | bytes 1048576 | tf_op jit(solution)/shard_map/pallas_call | solution.py:27
  30.7 8.1 %all-to-all-start = ((f32[32,4,128]{2,1,0:T(4,128)}), f32[32,4,128]{2,1,0:T(4,128)S(1)}, u32[]{:S(2)}, u32[]{:S(2)}) async-start(f32[32,4,128]{2,1,0:T(4,128)} %get-tuple-element.21), calls=%async_computation | async-start | bytes 131072 | tf_op jit(solution)/shard_map/all_to_all | solution.py:345
  38.8 3.6 %shard_map.97.counts = f32[256,2176]{1,0:T(8,128)S(1)} custom-call(s16[4,16,128]{2,1,0:T(8,128)(2,1)S(1)} %select_convert_fusion.refs_0_, s16[4,16,128]{2,1,0:T(8,128)(2,1)S(1)} %collective-permute-done.8.refs_1_, s16[4,16,128]{2,1,0:T(8,128)(2,1)S(1)} %collective-permute-done.9.refs_2_, s16[4,16,128]{2,1,0:T(8,128)(2,1)S(1)} %collective-permute-done.10.refs_3_, ...), custom_call_target="tpu_custom_call" | custom-call | flops 4294967296 | bytes 1048576 | tf_op jit(solution)/shard_map/pallas_call | solution.py:27
  42.4 1.4 %copy-done.2 = f32[256,2176]{1,0:T(8,128)} copy-done((f32[256,2176]{1,0:T(8,128)}, f32[256,2176]{1,0:T(8,128)S(1)}, u32[]{:S(2)}) %copy-start.2) | copy-done | bytes 2228248
  44.2 0.7 all-to-all-done.received
  44.8 1.6 %copy-done.3 = f32[256,2176]{1,0:T(8,128)S(1)} copy-done((f32[256,2176]{1,0:T(8,128)S(1)}, f32[256,2176]{1,0:T(8,128)}, u32[]{:S(2)}) %copy-start.3) | copy-done | bytes 2228248
  47.8 0.6 collective-permute-done.15.dscores
  49.6 1.3 %collective-permute-start.17 = (s16[168,256]{1,0:T(8,128)(2,1)S(1)}, s16[168,256]{1,0:T(8,128)(2,1)S(1)}, u32[]{:S(2)}, u32[]{:S(2)}) collective-permute-start(s16[168,256]{1,0:T(8,128)(2,1)S(1)} %get-tuple-element.30), channel_id=1, source_target_pairs={{0,2},{1,3},{2,0},{3,1},{4,6},{5,7},{6,4},{7,5},{8,10},{9,11},{10,... | collective-permute-start | bytes 258056 | tf_op jit(solution)/shard_map/ppermute | solution.py:294
  51.3 1.5 %collective-permute-start.19 = (s16[168,256]{1,0:T(8,128)(2,1)S(1)}, s16[168,256]{1,0:T(8,128)(2,1)S(1)}, u32[]{:S(2)}, u32[]{:S(2)}) collective-permute-start(s16[168,256]{1,0:T(8,128)(2,1)S(1)} %get-tuple-element.34), channel_id=1, source_target_pairs={{0,4},{1,5},{2,6},{3,7},{4,0},{5,1},{6,2},{7,3},{8,12},{9,13},{10,... | collective-permute-start | bytes 258056 | tf_op jit(solution)/shard_map/ppermute | solution.py:294
  52.8 1.1 %collective-permute-start.20 = (s16[168,256]{1,0:T(8,128)(2,1)S(1)}, s16[168,256]{1,0:T(8,128)(2,1)S(1)}, u32[]{:S(2)}, u32[]{:S(2)}) collective-permute-start(s16[168,256]{1,0:T(8,128)(2,1)S(1)} %get-tuple-element.35), channel_id=1, source_target_pairs={{0,5},{1,4},{2,7},{3,6},{4,1},{5,0},{6,3},{7,2},{8,13},{9,12},{10,... | collective-permute-start | bytes 258056 | tf_op jit(solution)/shard_map/ppermute | solution.py:294
  54.0 0.5 collective-permute-start.21
  54.5 1.2 %collective-permute-start.22 = (s16[168,256]{1,0:T(8,128)(2,1)S(1)}, s16[168,256]{1,0:T(8,128)(2,1)S(1)}, u32[]{:S(2)}, u32[]{:S(2)}) collective-permute-start(s16[168,256]{1,0:T(8,128)(2,1)S(1)} %get-tuple-element.37), channel_id=1, source_target_pairs={{0,7},{1,6},{2,5},{3,4},{4,3},{5,2},{6,1},{7,0},{8,15},{9,14},{10,... | collective-permute-start | bytes 258056 | tf_op jit(solution)/shard_map/ppermute | solution.py:294
  56.0 1.8 %collective-permute-done.19.refs_0_ = s16[168,256]{1,0:T(8,128)(2,1)S(1)} collective-permute-done((s16[168,256]{1,0:T(8,128)(2,1)S(1)}, s16[168,256]{1,0:T(8,128)(2,1)S(1)}, u32[]{:S(2)}, u32[]{:S(2)}) %collective-permute-start.19) | collective-permute-done | bytes 86048 | tf_op jit(solution)/shard_map/ppermute | solution.py:294
  57.8 6.1 %collective-permute-done.20.refs_1_ = s16[168,256]{1,0:T(8,128)(2,1)S(1)} collective-permute-done((s16[168,256]{1,0:T(8,128)(2,1)S(1)}, s16[168,256]{1,0:T(8,128)(2,1)S(1)}, u32[]{:S(2)}, u32[]{:S(2)}) %collective-permute-start.20) | collective-permute-done | bytes 86048 | tf_op jit(solution)/shard_map/ppermute | solution.py:294
  63.9 3.5 %collective-permute-done.21.refs_2_ = s16[168,256]{1,0:T(8,128)(2,1)S(1)} collective-permute-done((s16[168,256]{1,0:T(8,128)(2,1)S(1)}, s16[168,256]{1,0:T(8,128)(2,1)S(1)}, u32[]{:S(2)}, u32[]{:S(2)}) %collective-permute-start.21) | collective-permute-done | bytes 86048 | tf_op jit(solution)/shard_map/ppermute | solution.py:294
  67.4 2.1 %collective-permute-done.22.refs_3_ = s16[168,256]{1,0:T(8,128)(2,1)S(1)} collective-permute-done((s16[168,256]{1,0:T(8,128)(2,1)S(1)}, s16[168,256]{1,0:T(8,128)(2,1)S(1)}, u32[]{:S(2)}, u32[]{:S(2)}) %collective-permute-start.22) | collective-permute-done | bytes 86048 | tf_op jit(solution)/shard_map/ppermute | solution.py:294
  69.5 0.8 %shard_map.104 = (f32[160,512]{1,0:T(8,128)}, f32[2,64]{1,0:T(2,128)}) custom-call(f32[2,160,256]{2,1,0:T(8,128)S(1)} %get-tuple-element.32.sums_in, f32[2,2,256]{2,1,0:T(2,128)S(1)} %get-tuple-element.33.tops_in, s16[168,256]{1,0:T(8,128)(2,1)S(1)} %collective-permute-done.19.refs_0_, s16[168,256]{1,0:T(8,128)(2,1)S(1)} %collective-permute-done.20.refs_1_, ...), custom_call_target="tpu_custom_call" | custom-call | bytes 1048576 | tf_op jit(solution)/shard_map/pallas_call | solution.py:27
  (41 shorter events, 5.2 us)
Async XLA Ops:
  0.6 22.8 %collective-permute-start.2 = (bf16[160,512]{1,0:T(8,128)(2,1)}, bf16[160,512]{1,0:T(8,128)(2,1)S(1)}, u32[]{:S(2)}, u32[]{:S(2)}) collective-permute-start(bf16[160,512]{1,0:T(8,128)(2,1)} %refs_0_.1), channel_id=1, source_target_pairs={{0,2},{1,3},{2,0},{3,1},{4,6},{5,7},{6,4},{7,5},{8,10},{9,11},{10,... | collective-permute-start | bytes 491528 | tf_op jit(solution)/shard_map/ppermute | solution.py:294
  0.7 22.8 %collective-permute-start.4 = (bf16[160,512]{1,0:T(8,128)(2,1)}, bf16[160,512]{1,0:T(8,128)(2,1)S(1)}, u32[]{:S(2)}, u32[]{:S(2)}) collective-permute-start(bf16[160,512]{1,0:T(8,128)(2,1)} %refs_0_.1), channel_id=1, source_target_pairs={{0,6},{1,7},{2,4},{3,5},{4,2},{5,3},{6,0},{7,1},{8,14},{9,15},{10,... | collective-permute-start | bytes 491528 | tf_op jit(solution)/shard_map/ppermute | solution.py:294
  3.3 20.7 %collective-permute-start.6 = (bf16[160,512]{1,0:T(8,128)(2,1)}, bf16[160,512]{1,0:T(8,128)(2,1)S(1)}, u32[]{:S(2)}, u32[]{:S(2)}) collective-permute-start(bf16[160,512]{1,0:T(8,128)(2,1)} %refs_0_.1), channel_id=1, source_target_pairs={{0,4},{1,5},{2,6},{3,7},{4,0},{5,1},{6,2},{7,3},{8,12},{9,13},{10,... | collective-permute-start | bytes 491528 | tf_op jit(solution)/shard_map/ppermute | solution.py:294
  4.2 22.1 %collective-permute-start = (bf16[256,1280]{1,0:T(8,128)(2,1)}, bf16[256,1280]{1,0:T(8,128)(2,1)S(1)}, u32[]{:S(2)}, u32[]{:S(2)}) collective-permute-start(bf16[256,1280]{1,0:T(8,128)(2,1)} %own.5), channel_id=1, source_target_pairs={{0,1},{1,0},{2,3},{3,2},{4,5},{5,4},{6,7},{7,6},{8,9},{9,8},{10,11... | collective-permute-start | bytes 1966088 | tf_op jit(solution)/shard_map/ppermute | solution.py:294
  6.6 6.8 %collective-permute-start.9 = (s16[4,16,128]{2,1,0:T(8,128)(2,1)S(1)}, s16[4,16,128]{2,1,0:T(8,128)(2,1)S(1)}, u32[]{:S(2)}, u32[]{:S(2)}) collective-permute-start(s16[4,16,128]{2,1,0:T(8,128)(2,1)S(1)} %select_convert_fusion.refs_0_), channel_id=1, source_target_pairs={{0,2},{1,3},{2,0},{3,1},{4,6},{5,7},{6,4},{7,5},{8,10},{9,11},{10,... | collective-permute-start | bytes 49160 | tf_op jit(solution)/shard_map/ppermute | solution.py:294
  13.4 4.0 %collective-permute-start.11 = (s16[4,16,128]{2,1,0:T(8,128)(2,1)S(1)}, s16[4,16,128]{2,1,0:T(8,128)(2,1)S(1)}, u32[]{:S(2)}, u32[]{:S(2)}) collective-permute-start(s16[4,16,128]{2,1,0:T(8,128)(2,1)S(1)} %select_convert_fusion.refs_0_), channel_id=1, source_target_pairs={{0,4},{1,5},{2,6},{3,7},{4,0},{5,1},{6,2},{7,3},{8,12},{9,13},{10,... | collective-permute-start | bytes 49160 | tf_op jit(solution)/shard_map/ppermute | solution.py:294
  17.4 2.6 %collective-permute-start.13 = (s16[4,16,128]{2,1,0:T(8,128)(2,1)S(1)}, s16[4,16,128]{2,1,0:T(8,128)(2,1)S(1)}, u32[]{:S(2)}, u32[]{:S(2)}) collective-permute-start(s16[4,16,128]{2,1,0:T(8,128)(2,1)S(1)} %select_convert_fusion.refs_0_), channel_id=1, source_target_pairs={{0,6},{1,7},{2,4},{3,5},{4,2},{5,3},{6,0},{7,1},{8,14},{9,15},{10,... | collective-permute-start | bytes 49160 | tf_op jit(solution)/shard_map/ppermute | solution.py:294
  20.0 5.4 %collective-permute-start.1 = (bf16[160,512]{1,0:T(8,128)(2,1)}, bf16[160,512]{1,0:T(8,128)(2,1)S(1)}, u32[]{:S(2)}, u32[]{:S(2)}) collective-permute-start(bf16[160,512]{1,0:T(8,128)(2,1)} %refs_0_.1), channel_id=1, source_target_pairs={{0,1},{1,0},{2,3},{3,2},{4,5},{5,4},{6,7},{7,6},{8,9},{9,8},{10,11... | collective-permute-start | bytes 491528 | tf_op jit(solution)/shard_map/ppermute | solution.py:294
  23.5 2.4 %collective-permute-start.3 = (bf16[160,512]{1,0:T(8,128)(2,1)S(1)}, bf16[160,512]{1,0:T(8,128)(2,1)S(1)}, u32[]{:S(2)}, u32[]{:S(2)}) collective-permute-start(bf16[160,512]{1,0:T(8,128)(2,1)S(1)} %collective-permute-done.2.refs_2_), channel_id=1, source_target_pairs={{0,1},{1,0},{2,3},{3,2},{4,5},{5,4},{6,7},{7,6},{8,9},{9,8},{10,11... | collective-permute-start | bytes 491528 | tf_op jit(solution)/shard_map/ppermute | solution.py:294
  23.5 2.5 %collective-permute-start.5 = (bf16[160,512]{1,0:T(8,128)(2,1)S(1)}, bf16[160,512]{1,0:T(8,128)(2,1)S(1)}, u32[]{:S(2)}, u32[]{:S(2)}) collective-permute-start(bf16[160,512]{1,0:T(8,128)(2,1)S(1)} %collective-permute-done.4.refs_4_), channel_id=1, source_target_pairs={{0,1},{1,0},{2,3},{3,2},{4,5},{5,4},{6,7},{7,6},{8,9},{9,8},{10,11... | collective-permute-start | bytes 491528 | tf_op jit(solution)/shard_map/ppermute | solution.py:294
  24.0 5.1 %collective-permute-start.7 = (bf16[160,512]{1,0:T(8,128)(2,1)S(1)}, bf16[160,512]{1,0:T(8,128)(2,1)S(1)}, u32[]{:S(2)}, u32[]{:S(2)}) collective-permute-start(bf16[160,512]{1,0:T(8,128)(2,1)S(1)} %collective-permute-done.6.same), channel_id=1, source_target_pairs={{0,1},{1,0},{2,3},{3,2},{4,5},{5,4},{6,7},{7,6},{8,9},{9,8},{10,11... | collective-permute-start | bytes 491528 | tf_op jit(solution)/shard_map/ppermute | solution.py:294
  25.4 13.4 %collective-permute-start.8 = (s16[4,16,128]{2,1,0:T(8,128)(2,1)S(1)}, s16[4,16,128]{2,1,0:T(8,128)(2,1)S(1)}, u32[]{:S(2)}, u32[]{:S(2)}) collective-permute-start(s16[4,16,128]{2,1,0:T(8,128)(2,1)S(1)} %select_convert_fusion.refs_0_), channel_id=1, source_target_pairs={{0,1},{1,0},{2,3},{3,2},{4,5},{5,4},{6,7},{7,6},{8,9},{9,8},{10,11... | collective-permute-start | bytes 49160 | tf_op jit(solution)/shard_map/ppermute | solution.py:294
  25.9 12.9 %collective-permute-start.10 = (s16[4,16,128]{2,1,0:T(8,128)(2,1)S(1)}, s16[4,16,128]{2,1,0:T(8,128)(2,1)S(1)}, u32[]{:S(2)}, u32[]{:S(2)}) collective-permute-start(s16[4,16,128]{2,1,0:T(8,128)(2,1)S(1)} %collective-permute-done.9.refs_2_), channel_id=1, source_target_pairs={{0,1},{1,0},{2,3},{3,2},{4,5},{5,4},{6,7},{7,6},{8,9},{9,8},{10,11... | collective-permute-start | bytes 49160 | tf_op jit(solution)/shard_map/ppermute | solution.py:294
  26.0 12.9 %collective-permute-start.12 = (s16[4,16,128]{2,1,0:T(8,128)(2,1)S(1)}, s16[4,16,128]{2,1,0:T(8,128)(2,1)S(1)}, u32[]{:S(2)}, u32[]{:S(2)}) collective-permute-start(s16[4,16,128]{2,1,0:T(8,128)(2,1)S(1)} %collective-permute-done.11.refs_4_), channel_id=1, source_target_pairs={{0,1},{1,0},{2,3},{3,2},{4,5},{5,4},{6,7},{7,6},{8,9},{9,8},{10,11... | collective-permute-start | bytes 49160 | tf_op jit(solution)/shard_map/ppermute | solution.py:294
  26.4 12.4 %collective-permute-start.14 = (s16[4,16,128]{2,1,0:T(8,128)(2,1)S(1)}, s16[4,16,128]{2,1,0:T(8,128)(2,1)S(1)}, u32[]{:S(2)}, u32[]{:S(2)}) collective-permute-start(s16[4,16,128]{2,1,0:T(8,128)(2,1)S(1)} %collective-permute-done.13.refs_6_), channel_id=1, source_target_pairs={{0,1},{1,0},{2,3},{3,2},{4,5},{5,4},{6,7},{7,6},{8,9},{9,8},{10,11... | collective-permute-start | bytes 49160 | tf_op jit(solution)/shard_map/ppermute | solution.py:294
  26.5 1.1 %copy-start = (bf16[256,1280]{1,0:T(8,128)(2,1)S(1)}, bf16[256,1280]{1,0:T(8,128)(2,1)}, u32[]{:S(2)}) copy-start(bf16[256,1280]{1,0:T(8,128)(2,1)} %own.5) | copy-start | bytes 1966084
  27.6 0.9 %copy-start.4 = (bf16[160,512]{1,0:T(8,128)(2,1)S(1)}, bf16[160,512]{1,0:T(8,128)(2,1)}, u32[]{:S(2)}) copy-start(bf16[160,512]{1,0:T(8,128)(2,1)} %refs_0_.1) | copy-start | bytes 491524
  30.7 14.2 %all-to-all-start = ((f32[32,4,128]{2,1,0:T(4,128)}), f32[32,4,128]{2,1,0:T(4,128)S(1)}, u32[]{:S(2)}, u32[]{:S(2)}) async-start(f32[32,4,128]{2,1,0:T(4,128)} %get-tuple-element.21), calls=%async_computation | async-start | bytes 131072 | tf_op jit(solution)/shard_map/all_to_all | solution.py:345
  38.8 5.0 %copy-start.1 = (bf16[256,1280]{1,0:T(8,128)(2,1)S(1)}, bf16[256,1280]{1,0:T(8,128)(2,1)}, u32[]{:S(2)}) copy-start(bf16[256,1280]{1,0:T(8,128)(2,1)} %own.5) | copy-start | bytes 1966084
  42.4 1.4 %copy-start.2 = (f32[256,2176]{1,0:T(8,128)}, f32[256,2176]{1,0:T(8,128)S(1)}, u32[]{:S(2)}) copy-start(f32[256,2176]{1,0:T(8,128)S(1)} %shard_map.97.counts) | copy-start | bytes 6684676
  44.8 1.6 %copy-start.3 = (f32[256,2176]{1,0:T(8,128)S(1)}, f32[256,2176]{1,0:T(8,128)}, u32[]{:S(2)}) copy-start(f32[256,2176]{1,0:T(8,128)} %copy-done.2) | copy-start | bytes 6684676
  47.0 1.4 %collective-permute-start.15 = (f32[256,1]{1,0:T(8,128)S(1)}, f32[256,1]{1,0:T(8,128)S(1)}, u32[]{:S(2)}, u32[]{:S(2)}) collective-permute-start(f32[256,1]{1,0:T(8,128)S(1)} %shard_map.98.dscores), channel_id=1, source_target_pairs={{0,1},{1,0},{2,3},{3,2},{4,5},{5,4},{6,7},{7,6},{8,9},{9,8},{10,11... | collective-permute-start | bytes 3080 | tf_op jit(solution)/shard_map/ppermute | solution.py:294
  49.1 4.8 %collective-permute-start.16 = (s16[168,256]{1,0:T(8,128)(2,1)S(1)}, s16[168,256]{1,0:T(8,128)(2,1)S(1)}, u32[]{:S(2)}, u32[]{:S(2)}) collective-permute-start(s16[168,256]{1,0:T(8,128)(2,1)S(1)} %get-tuple-element.29), channel_id=1, source_target_pairs={{0,1},{1,0},{2,3},{3,2},{4,5},{5,4},{6,7},{7,6},{8,9},{9,8},{10,11... | collective-permute-start | bytes 258056 | tf_op jit(solution)/shard_map/ppermute | solution.py:294
  49.6 4.9 %collective-permute-start.17 = (s16[168,256]{1,0:T(8,128)(2,1)S(1)}, s16[168,256]{1,0:T(8,128)(2,1)S(1)}, u32[]{:S(2)}, u32[]{:S(2)}) collective-permute-start(s16[168,256]{1,0:T(8,128)(2,1)S(1)} %get-tuple-element.30), channel_id=1, source_target_pairs={{0,2},{1,3},{2,0},{3,1},{4,6},{5,7},{6,4},{7,5},{8,10},{9,11},{10,... | collective-permute-start | bytes 258056 | tf_op jit(solution)/shard_map/ppermute | solution.py:294
  50.9 5.0 %collective-permute-start.18 = (s16[168,256]{1,0:T(8,128)(2,1)S(1)}, s16[168,256]{1,0:T(8,128)(2,1)S(1)}, u32[]{:S(2)}, u32[]{:S(2)}) collective-permute-start(s16[168,256]{1,0:T(8,128)(2,1)S(1)} %get-tuple-element.31), channel_id=1, source_target_pairs={{0,3},{1,2},{2,1},{3,0},{4,7},{5,6},{6,5},{7,4},{8,11},{9,10},{10,... | collective-permute-start | bytes 258056 | tf_op jit(solution)/shard_map/ppermute | solution.py:294
  51.3 6.5 %collective-permute-start.19 = (s16[168,256]{1,0:T(8,128)(2,1)S(1)}, s16[168,256]{1,0:T(8,128)(2,1)S(1)}, u32[]{:S(2)}, u32[]{:S(2)}) collective-permute-start(s16[168,256]{1,0:T(8,128)(2,1)S(1)} %get-tuple-element.34), channel_id=1, source_target_pairs={{0,4},{1,5},{2,6},{3,7},{4,0},{5,1},{6,2},{7,3},{8,12},{9,13},{10,... | collective-permute-start | bytes 258056 | tf_op jit(solution)/shard_map/ppermute | solution.py:294
  52.8 11.1 %collective-permute-start.20 = (s16[168,256]{1,0:T(8,128)(2,1)S(1)}, s16[168,256]{1,0:T(8,128)(2,1)S(1)}, u32[]{:S(2)}, u32[]{:S(2)}) collective-permute-start(s16[168,256]{1,0:T(8,128)(2,1)S(1)} %get-tuple-element.35), channel_id=1, source_target_pairs={{0,5},{1,4},{2,7},{3,6},{4,1},{5,0},{6,3},{7,2},{8,13},{9,12},{10,... | collective-permute-start | bytes 258056 | tf_op jit(solution)/shard_map/ppermute | solution.py:294
  54.0 13.5 %collective-permute-start.21 = (s16[168,256]{1,0:T(8,128)(2,1)S(1)}, s16[168,256]{1,0:T(8,128)(2,1)S(1)}, u32[]{:S(2)}, u32[]{:S(2)}) collective-permute-start(s16[168,256]{1,0:T(8,128)(2,1)S(1)} %get-tuple-element.36), channel_id=1, source_target_pairs={{0,6},{1,7},{2,4},{3,5},{4,2},{5,3},{6,0},{7,1},{8,14},{9,15},{10,... | collective-permute-start | bytes 258056 | tf_op jit(solution)/shard_map/ppermute | solution.py:294
  54.5 15.0 %collective-permute-start.22 = (s16[168,256]{1,0:T(8,128)(2,1)S(1)}, s16[168,256]{1,0:T(8,128)(2,1)S(1)}, u32[]{:S(2)}, u32[]{:S(2)}) collective-permute-start(s16[168,256]{1,0:T(8,128)(2,1)S(1)} %get-tuple-element.37), channel_id=1, source_target_pairs={{0,7},{1,6},{2,5},{3,4},{4,3},{5,2},{6,1},{7,0},{8,15},{9,14},{10,... | collective-permute-start | bytes 258056 | tf_op jit(solution)/shard_map/ppermute | solution.py:294

commit v3 on v2

--- a/solution.py
+++ b/solution.py
@@ -12,6 +12,7 @@
 BF16 = jnp.bfloat16
 LANES = 128
 TAIL = 8
+SCALE = 0.7978845608028654
 NT = (((1,), (1,)), ((), ()))
 
 
@@ -105,7 +106,7 @@
         out[pl.ds(at, rows), :] = jnp.dot(ref[...], gathered[...], preferred_element_type=F32)
 
 
-def forward_kernel(late, own, partner, bias, w_out, begun, same, other, score, hidden, slope, gathered):
+def forward_kernel(late, own, partner, bias, w_out, begun, same, other, score, hidden, kept, gathered):
     shard = lax.axis_index("shard")
     core = shard % 2
     rows = own.shape[0]
@@ -125,14 +126,10 @@
         at = pl.multiple_of((core ^ j) * rows, rows)
         late_part = jnp.dot(ref[:, pl.ds(tile, window)], gathered[...], preferred_element_type=F32)
         pre = (begun[pl.ds(at, rows), :] + late_part) + shift
-        square = pre * pre
-        scale = 0.7978845608028654
-        t = jnp.tanh(scale * (pre + 0.044715 * (square * pre)))
+        kept[pl.ds(at, rows), :] = pre
+        t = jnp.tanh(SCALE * (pre + 0.044715 * (pre * pre * pre)))
         out = (pre * (0.5 * (1.0 + t))).astype(BF16)
         hidden[pl.ds(at, rows), :] = out
-        slope[pl.ds(at, rows), :] = 0.5 * (1.0 + t) + (0.5 * pre) * (1.0 - t * t) * (
-            scale * (1.0 + (3.0 * 0.044715) * square)
-        )
         part = lax.dot_general(
             jnp.broadcast_to(weights, (8, half)), out, NT, preferred_element_type=F32
         )
@@ -186,6 +183,12 @@
         dscore[span, :] = jnp.sum(total, axis=1, keepdims=True)
 
 
+def slope_of(pre):
+    square = pre * pre
+    t = jnp.tanh(SCALE * (pre + 0.044715 * (square * pre)))
+    return 0.5 * (1.0 + t) + (0.5 * pre) * (1.0 - t * t) * (SCALE * (1.0 + (3.0 * 0.044715) * square))
+
+
 def dpre_of(dscores, rows_at, hidden, slope, weights, sent):
     half = hidden.shape[1]
     bias_sum, score_sum = jnp.zeros((1, half), F32), jnp.zeros((1, half), F32)
@@ -193,7 +196,7 @@
         span = slice(r * LANES, (r + 1) * LANES)
         there = pl.ds(pl.multiple_of(rows_at + r * LANES, LANES), LANES)
         dscore = dscores[span, :]
-        dpre = (dscore * weights) * slope[there, :]
+        dpre = (dscore * weights) * slope(span, there)
         bias_sum = bias_sum + jnp.sum(dpre, axis=0, keepdims=True)
         score_sum = score_sum + jnp.sum(dscore * hidden[there, :].astype(F32), axis=0, keepdims=True)
         sent[span, :] = dpre.astype(BF16)
@@ -205,11 +208,13 @@
     return w_out[:, pl.ds(pl.multiple_of(core * half, half), half)].astype(F32)
 
 
-def own_kernel(dscores, flipped, hidden, slope, w_out, terms, sums, sent):
+def own_kernel(dscores, flipped, hidden, pre, w_out, terms, sums, slope, sent):
     core = lax.axis_index("shard") % 2
     rows = dscores.shape[0]
     at = pl.multiple_of(core * rows, rows)
-    sums[...] = dpre_of(dscores, at, hidden, slope, weights_of(w_out, hidden.shape[1]), sent)
+    weights = weights_of(w_out, hidden.shape[1])
+    sums[...] = dpre_of(dscores, at, hidden, lambda _, there: slope_of(pre[there, :]), weights, sent)
+    slope[...] = slope_of(pre[pl.ds(pl.multiple_of((1 - core) * rows, rows), rows), :])
     terms[...] = jnp.dot(flipped[:, pl.ds(at, rows)], sent[...], preferred_element_type=F32)
 
 
@@ -234,7 +239,8 @@
 def far_kernel(first, dscores, own_terms, own_sums, flipped, hidden, slope, w_out, heads, sent, *messages):
     core = lax.axis_index("shard") % 2
     at = (1 - core) * dscores.shape[0]
-    sums = dpre_of(dscores, at, hidden, slope, weights_of(w_out, hidden.shape[1]), sent)
+    weights = weights_of(w_out, hidden.shape[1])
+    sums = dpre_of(dscores, at, hidden, lambda span, _: slope[span, :], weights, sent)
     heads[...] = own_sums[...] + sums
     for m, ref in enumerate(messages, first):
         write_message(ref, block_of(m, flipped, own_terms, sent, ref.shape[0] - TAIL), heads[...])
@@ -331,7 +337,7 @@
         [pltpu.VMEM((channels, half), BF16)],
         flops=3 * rows * channels * half,
     )
-    score, hidden, slope = call(
+    score, hidden, pre = call(
         functools.partial(forward_kernel, late),
         (embeddings, partner, bias, w_out, begun, blocks[late], blocks[late + 1]),
         [
@@ -349,10 +355,10 @@
     next_to = swap(near, 1)
     message = shape((depth + TAIL, half), jnp.int16)
     first = n // 2
-    own_terms, own_sums = call(
+    own_terms, own_sums, slope = call(
         own_kernel,
-        (near, flipped, hidden, slope, w_out),
-        [shape((channels, half), F32), shape((2, half), F32)],
+        (near, flipped, hidden, pre, w_out),
+        [shape((channels, half), F32), shape((2, half), F32), shape((rows, half), F32)],
         [pltpu.VMEM((rows, half), BF16)],
         flops=2 * rows * channels * half,
     )

time: 70.7 us -> 70.5 us (level)
  transfers between devices with their start and end apart: 24 -> 24, of which waited for: 10 -> 10; matrix products, arithmetic and copies ran while one was open for 3% -> 3% of each run, Pallas kernels for 9% -> 10%
where the time goes in v3:
time: 70.5 us; the launch traced here: 70.2 us
  waiting for transfers between devices  26.7 us (38%)
  starting transfers between devices  26.6 us (38%)
  Pallas kernels  8.89 us (13%)
  local copies, waits for them, and re-layouts  6.39 us (9%)
  other arithmetic  0.84 us (1%)
  between operations  0.79 us (1%)
    ppermute x23, waiting for transfers between devices, swap(): return lax.ppermute(value, 'shard', [(i, i ^ m) for i in range(n)])  26.1 us
    ppermute x23, starting transfers between devices, swap(): return lax.ppermute(value, 'shard', [(i, i ^ m) for i in range(n)])  18.5 us
    pallas_call x10, Pallas kernels, call(): pl.pallas_call(body, out_shape=outputs, in_specs=[pl.BlockSpec(memory_spa...  8.89 us
    all_to_all x1, starting transfers between devices, by_ppermute(): received = lax.all_to_all(score, ('grp', 'shard'), 0, 0, tiled=True)  8.1 us
    unnamed x10, local copies, waits for them, and re-layouts  5.02 us
  transfers between devices with their start and end apart: 24, of which 10 were waited for; matrix products, arithmetic and copies ran while one was open for 3% of the time, Pallas kernels for 10%

profile of v3, /device:TPU:9, one launch (start us, length us, event | category | flops | bytes accessed | tf_op | source)
XLA Modules:
  0.0 70.2 jit_solution(10704504094890209050)
XLA Ops:
  0.7 2.6 %collective-permute-start.4 = (bf16[160,512]{1,0:T(8,128)(2,1)}, bf16[160,512]{1,0:T(8,128)(2,1)S(1)}, u32[]{:S(2)}, u32[]{:S(2)}) collective-permute-start(bf16[160,512]{1,0:T(8,128)(2,1)} %refs_0_.1), channel_id=1, source_target_pairs={{0,6},{1,7},{2,4},{3,5},{4,2},{5,3},{6,0},{7,1},{8,14},{9,15},{10,... | collective-permute-start | bytes 491528 | tf_op jit(solution)/shard_map/ppermute | solution.py:300
  3.3 1.0 %collective-permute-start.6 = (bf16[160,512]{1,0:T(8,128)(2,1)}, bf16[160,512]{1,0:T(8,128)(2,1)S(1)}, u32[]{:S(2)}, u32[]{:S(2)}) collective-permute-start(bf16[160,512]{1,0:T(8,128)(2,1)} %refs_0_.1), channel_id=1, source_target_pairs={{0,4},{1,5},{2,6},{3,7},{4,0},{5,1},{6,2},{7,3},{8,12},{9,13},{10,... | collective-permute-start | bytes 491528 | tf_op jit(solution)/shard_map/ppermute | solution.py:300
  4.2 1.5 %collective-permute-start = (bf16[256,1280]{1,0:T(8,128)(2,1)}, bf16[256,1280]{1,0:T(8,128)(2,1)S(1)}, u32[]{:S(2)}, u32[]{:S(2)}) collective-permute-start(bf16[256,1280]{1,0:T(8,128)(2,1)} %own.5), channel_id=1, source_target_pairs={{0,1},{1,0},{2,3},{3,2},{4,5},{5,4},{6,7},{7,6},{8,9},{9,8},{10,11... | collective-permute-start | bytes 1966088 | tf_op jit(solution)/shard_map/ppermute | solution.py:300
  5.8 0.8 %select_convert_fusion.refs_0_ = s16[4,16,128]{2,1,0:T(8,128)(2,1)S(1)} fusion(s32[16,128]{1,0:T(8,128)} %bitcast.5, s32[16,128]{1,0:T(8,128)} %bitcast.6, s32[16,128]{1,0:T(8,128)} %bitcast.7, s32[16,128]{1,0:T(8,128)} %bitcast.8, pred[4]{0:T(512)(128)(4,1)S(1)} %get-tuple-element.42, pred[4]{0:T(512)(128)(4,1)S(1)} %get-tuple-element.43, ...), kind=kLoop, calls=%fused_computation | loop fusion | flops 32768 | bytes 49164 | tf_op jit(solution)/shard_map/convert_element_type | solution.py:319
  6.7 6.7 %collective-permute-done.9.refs_2_ = s16[4,16,128]{2,1,0:T(8,128)(2,1)S(1)} collective-permute-done((s16[4,16,128]{2,1,0:T(8,128)(2,1)S(1)}, s16[4,16,128]{2,1,0:T(8,128)(2,1)S(1)}, u32[]{:S(2)}, u32[]{:S(2)}) %collective-permute-start.9) | collective-permute-done | bytes 16416 | tf_op jit(solution)/shard_map/ppermute | solution.py:300
  13.7 3.7 %collective-permute-done.11.refs_4_ = s16[4,16,128]{2,1,0:T(8,128)(2,1)S(1)} collective-permute-done((s16[4,16,128]{2,1,0:T(8,128)(2,1)S(1)}, s16[4,16,128]{2,1,0:T(8,128)(2,1)S(1)}, u32[]{:S(2)}, u32[]{:S(2)}) %collective-permute-start.11) | collective-permute-done | bytes 16416 | tf_op jit(solution)/shard_map/ppermute | solution.py:300
  17.4 0.9 %collective-permute-start.13 = (s16[4,16,128]{2,1,0:T(8,128)(2,1)S(1)}, s16[4,16,128]{2,1,0:T(8,128)(2,1)S(1)}, u32[]{:S(2)}, u32[]{:S(2)}) collective-permute-start(s16[4,16,128]{2,1,0:T(8,128)(2,1)S(1)} %select_convert_fusion.refs_0_), channel_id=1, source_target_pairs={{0,6},{1,7},{2,4},{3,5},{4,2},{5,3},{6,0},{7,1},{8,14},{9,15},{10,... | collective-permute-start | bytes 49160 | tf_op jit(solution)/shard_map/ppermute | solution.py:300
  18.3 1.7 %collective-permute-done.13.refs_6_ = s16[4,16,128]{2,1,0:T(8,128)(2,1)S(1)} collective-permute-done((s16[4,16,128]{2,1,0:T(8,128)(2,1)S(1)}, s16[4,16,128]{2,1,0:T(8,128)(2,1)S(1)}, u32[]{:S(2)}, u32[]{:S(2)}) %collective-permute-start.13) | collective-permute-done | bytes 16416 | tf_op jit(solution)/shard_map/ppermute | solution.py:300
  20.0 3.5 %collective-permute-start.1 = (bf16[160,512]{1,0:T(8,128)(2,1)}, bf16[160,512]{1,0:T(8,128)(2,1)S(1)}, u32[]{:S(2)}, u32[]{:S(2)}) collective-permute-start(bf16[160,512]{1,0:T(8,128)(2,1)} %refs_0_.1), channel_id=1, source_target_pairs={{0,1},{1,0},{2,3},{3,2},{4,5},{5,4},{6,7},{7,6},{8,9},{9,8},{10,11... | collective-permute-start | bytes 491528 | tf_op jit(solution)/shard_map/ppermute | solution.py:300
  23.5 0.5 collective-permute-start.5
  24.1 0.7 reshape.18.bias
  24.7 0.7 reshape.19.w_out
  26.5 1.1 %copy-done = bf16[256,1280]{1,0:T(8,128)(2,1)S(1)} copy-done((bf16[256,1280]{1,0:T(8,128)(2,1)S(1)}, bf16[256,1280]{1,0:T(8,128)(2,1)}, u32[]{:S(2)}) %copy-start) | copy-done | bytes 655384
  27.6 0.9 %copy-done.4 = bf16[160,512]{1,0:T(8,128)(2,1)S(1)} copy-done((bf16[160,512]{1,0:T(8,128)(2,1)S(1)}, bf16[160,512]{1,0:T(8,128)(2,1)}, u32[]{:S(2)}) %copy-start.4) | copy-done | bytes 163864
  28.5 0.6 shard_map.95.begun
  29.0 1.5 %shard_map.96 = (f32[32,4,128]{2,1,0:T(4,128)}, bf16[512,256]{1,0:T(8,128)(2,1)S(1)}, f32[512,256]{1,0:T(8,128)S(1)}) custom-call(bf16[256,1280]{1,0:T(8,128)(2,1)S(1)} %copy-done, bf16[256,1280]{1,0:T(8,128)(2,1)S(1)} %collective-permute-done.partner, bf16[1,512]{1,0:T(2,128)(2,1)S(1)} %reshape.18.bias, bf16[1,512]{1,0:T(2,128)(2,1)S(1)} %reshape.19.w_out, ...), custom_call_target="tpu_custom_call" | custom-call | flops 83886080 | bytes 1048576 | tf_op jit(solution)/shard_map/pallas_call | solution.py:28
  30.5 8.1 %all-to-all-start = ((f32[32,4,128]{2,1,0:T(4,128)}), f32[32,4,128]{2,1,0:T(4,128)S(1)}, u32[]{:S(2)}, u32[]{:S(2)}) async-start(f32[32,4,128]{2,1,0:T(4,128)} %get-tuple-element.22), calls=%async_computation | async-start | bytes 131072 | tf_op jit(solution)/shard_map/all_to_all | solution.py:351
  38.7 3.6 %shard_map.97.counts = f32[256,2176]{1,0:T(8,128)S(1)} custom-call(s16[4,16,128]{2,1,0:T(8,128)(2,1)S(1)} %select_convert_fusion.refs_0_, s16[4,16,128]{2,1,0:T(8,128)(2,1)S(1)} %collective-permute-done.8.refs_1_, s16[4,16,128]{2,1,0:T(8,128)(2,1)S(1)} %collective-permute-done.9.refs_2_, s16[4,16,128]{2,1,0:T(8,128)(2,1)S(1)} %collective-permute-done.10.refs_3_, ...), custom_call_target="tpu_custom_call" | custom-call | flops 4294967296 | bytes 1048576 | tf_op jit(solution)/shard_map/pallas_call | solution.py:28
  42.3 1.4 %copy-done.2 = f32[256,2176]{1,0:T(8,128)} copy-done((f32[256,2176]{1,0:T(8,128)}, f32[256,2176]{1,0:T(8,128)S(1)}, u32[]{:S(2)}) %copy-start.2) | copy-done | bytes 2228248
  44.0 0.7 all-to-all-done.received
  44.7 1.6 %copy-done.3 = f32[256,2176]{1,0:T(8,128)S(1)} copy-done((f32[256,2176]{1,0:T(8,128)S(1)}, f32[256,2176]{1,0:T(8,128)}, u32[]{:S(2)}) %copy-start.3) | copy-done | bytes 2228248
  47.2 0.7 %shard_map.100 = (f32[1280,256]{1,0:T(8,128)S(1)}, f32[2,256]{1,0:T(2,128)S(1)}, f32[256,256]{1,0:T(8,128)S(1)}) custom-call(f32[256,1]{1,0:T(8,128)S(1)} %shard_map.98.dscores, bf16[1280,512]{1,0:T(8,128)(2,1)S(1)} %shard_map.99.flipped, bf16[512,256]{1,0:T(8,128)(2,1)S(1)} %get-tuple-element.23.hidden, f32[512,256]{1,0:T(8,128)S(1)} %get-tuple-element.24.pre, ...), custom_call_target="tpu_custom_call" | custom-call | flops 167772160 | bytes 1048576 | tf_op jit(solution)/shard_map/pallas_call | solution.py:28
  49.4 1.3 %collective-permute-start.17 = (s16[168,256]{1,0:T(8,128)(2,1)S(1)}, s16[168,256]{1,0:T(8,128)(2,1)S(1)}, u32[]{:S(2)}, u32[]{:S(2)}) collective-permute-start(s16[168,256]{1,0:T(8,128)(2,1)S(1)} %get-tuple-element.32), channel_id=1, source_target_pairs={{0,2},{1,3},{2,0},{3,1},{4,6},{5,7},{6,4},{7,5},{8,10},{9,11},{10,... | collective-permute-start | bytes 258056 | tf_op jit(solution)/shard_map/ppermute | solution.py:300
  51.2 1.5 %collective-permute-start.19 = (s16[168,256]{1,0:T(8,128)(2,1)S(1)}, s16[168,256]{1,0:T(8,128)(2,1)S(1)}, u32[]{:S(2)}, u32[]{:S(2)}) collective-permute-start(s16[168,256]{1,0:T(8,128)(2,1)S(1)} %get-tuple-element.36), channel_id=1, source_target_pairs={{0,4},{1,5},{2,6},{3,7},{4,0},{5,1},{6,2},{7,3},{8,12},{9,13},{10,... | collective-permute-start | bytes 258056 | tf_op jit(solution)/shard_map/ppermute | solution.py:300
  52.7 1.1 %collective-permute-start.20 = (s16[168,256]{1,0:T(8,128)(2,1)S(1)}, s16[168,256]{1,0:T(8,128)(2,1)S(1)}, u32[]{:S(2)}, u32[]{:S(2)}) collective-permute-start(s16[168,256]{1,0:T(8,128)(2,1)S(1)} %get-tuple-element.37), channel_id=1, source_target_pairs={{0,5},{1,4},{2,7},{3,6},{4,1},{5,0},{6,3},{7,2},{8,13},{9,12},{10,... | collective-permute-start | bytes 258056 | tf_op jit(solution)/shard_map/ppermute | solution.py:300
  53.8 0.5 collective-permute-start.21
  54.4 1.2 %collective-permute-start.22 = (s16[168,256]{1,0:T(8,128)(2,1)S(1)}, s16[168,256]{1,0:T(8,128)(2,1)S(1)}, u32[]{:S(2)}, u32[]{:S(2)}) collective-permute-start(s16[168,256]{1,0:T(8,128)(2,1)S(1)} %get-tuple-element.39), channel_id=1, source_target_pairs={{0,7},{1,6},{2,5},{3,4},{4,3},{5,2},{6,1},{7,0},{8,15},{9,14},{10,... | collective-permute-start | bytes 258056 | tf_op jit(solution)/shard_map/ppermute | solution.py:300
  55.8 1.8 %collective-permute-done.19.refs_0_ = s16[168,256]{1,0:T(8,128)(2,1)S(1)} collective-permute-done((s16[168,256]{1,0:T(8,128)(2,1)S(1)}, s16[168,256]{1,0:T(8,128)(2,1)S(1)}, u32[]{:S(2)}, u32[]{:S(2)}) %collective-permute-start.19) | collective-permute-done | bytes 86048 | tf_op jit(solution)/shard_map/ppermute | solution.py:300
  57.7 6.1 %collective-permute-done.20.refs_1_ = s16[168,256]{1,0:T(8,128)(2,1)S(1)} collective-permute-done((s16[168,256]{1,0:T(8,128)(2,1)S(1)}, s16[168,256]{1,0:T(8,128)(2,1)S(1)}, u32[]{:S(2)}, u32[]{:S(2)}) %collective-permute-start.20) | collective-permute-done | bytes 86048 | tf_op jit(solution)/shard_map/ppermute | solution.py:300
  63.8 3.5 %collective-permute-done.21.refs_2_ = s16[168,256]{1,0:T(8,128)(2,1)S(1)} collective-permute-done((s16[168,256]{1,0:T(8,128)(2,1)S(1)}, s16[168,256]{1,0:T(8,128)(2,1)S(1)}, u32[]{:S(2)}, u32[]{:S(2)}) %collective-permute-start.21) | collective-permute-done | bytes 86048 | tf_op jit(solution)/shard_map/ppermute | solution.py:300
  67.3 2.1 %collective-permute-done.22.refs_3_ = s16[168,256]{1,0:T(8,128)(2,1)S(1)} collective-permute-done((s16[168,256]{1,0:T(8,128)(2,1)S(1)}, s16[168,256]{1,0:T(8,128)(2,1)S(1)}, u32[]{:S(2)}, u32[]{:S(2)}) %collective-permute-start.22) | collective-permute-done | bytes 86048 | tf_op jit(solution)/shard_map/ppermute | solution.py:300
  69.4 0.8 %shard_map.104 = (f32[160,512]{1,0:T(8,128)}, f32[2,64]{1,0:T(2,128)}) custom-call(f32[2,160,256]{2,1,0:T(8,128)S(1)} %get-tuple-element.34.sums_in, f32[2,2,256]{2,1,0:T(2,128)S(1)} %get-tuple-element.35.tops_in, s16[168,256]{1,0:T(8,128)(2,1)S(1)} %collective-permute-done.19.refs_0_, s16[168,256]{1,0:T(8,128)(2,1)S(1)} %collective-permute-done.20.refs_1_, ...), custom_call_target="tpu_custom_call" | custom-call | bytes 1048576 | tf_op jit(solution)/shard_map/pallas_call | solution.py:28
  (41 shorter events, 5.0 us)
Async XLA Ops:
  0.6 22.8 %collective-permute-start.2 = (bf16[160,512]{1,0:T(8,128)(2,1)}, bf16[160,512]{1,0:T(8,128)(2,1)S(1)}, u32[]{:S(2)}, u32[]{:S(2)}) collective-permute-start(bf16[160,512]{1,0:T(8,128)(2,1)} %refs_0_.1), channel_id=1, source_target_pairs={{0,2},{1,3},{2,0},{3,1},{4,6},{5,7},{6,4},{7,5},{8,10},{9,11},{10,... | collective-permute-start | bytes 491528 | tf_op jit(solution)/shard_map/ppermute | solution.py:300
  0.7 22.8 %collective-permute-start.4 = (bf16[160,512]{1,0:T(8,128)(2,1)}, bf16[160,512]{1,0:T(8,128)(2,1)S(1)}, u32[]{:S(2)}, u32[]{:S(2)}) collective-permute-start(bf16[160,512]{1,0:T(8,128)(2,1)} %refs_0_.1), channel_id=1, source_target_pairs={{0,6},{1,7},{2,4},{3,5},{4,2},{5,3},{6,0},{7,1},{8,14},{9,15},{10,... | collective-permute-start | bytes 491528 | tf_op jit(solution)/shard_map/ppermute | solution.py:300
  3.3 20.7 %collective-permute-start.6 = (bf16[160,512]{1,0:T(8,128)(2,1)}, bf16[160,512]{1,0:T(8,128)(2,1)S(1)}, u32[]{:S(2)}, u32[]{:S(2)}) collective-permute-start(bf16[160,512]{1,0:T(8,128)(2,1)} %refs_0_.1), channel_id=1, source_target_pairs={{0,4},{1,5},{2,6},{3,7},{4,0},{5,1},{6,2},{7,3},{8,12},{9,13},{10,... | collective-permute-start | bytes 491528 | tf_op jit(solution)/shard_map/ppermute | solution.py:300
  4.2 22.1 %collective-permute-start = (bf16[256,1280]{1,0:T(8,128)(2,1)}, bf16[256,1280]{1,0:T(8,128)(2,1)S(1)}, u32[]{:S(2)}, u32[]{:S(2)}) collective-permute-start(bf16[256,1280]{1,0:T(8,128)(2,1)} %own.5), channel_id=1, source_target_pairs={{0,1},{1,0},{2,3},{3,2},{4,5},{5,4},{6,7},{7,6},{8,9},{9,8},{10,11... | collective-permute-start | bytes 1966088 | tf_op jit(solution)/shard_map/ppermute | solution.py:300
  6.6 6.8 %collective-permute-start.9 = (s16[4,16,128]{2,1,0:T(8,128)(2,1)S(1)}, s16[4,16,128]{2,1,0:T(8,128)(2,1)S(1)}, u32[]{:S(2)}, u32[]{:S(2)}) collective-permute-start(s16[4,16,128]{2,1,0:T(8,128)(2,1)S(1)} %select_convert_fusion.refs_0_), channel_id=1, source_target_pairs={{0,2},{1,3},{2,0},{3,1},{4,6},{5,7},{6,4},{7,5},{8,10},{9,11},{10,... | collective-permute-start | bytes 49160 | tf_op jit(solution)/shard_map/ppermute | solution.py:300
  13.4 4.0 %collective-permute-start.11 = (s16[4,16,128]{2,1,0:T(8,128)(2,1)S(1)}, s16[4,16,128]{2,1,0:T(8,128)(2,1)S(1)}, u32[]{:S(2)}, u32[]{:S(2)}) collective-permute-start(s16[4,16,128]{2,1,0:T(8,128)(2,1)S(1)} %select_convert_fusion.refs_0_), channel_id=1, source_target_pairs={{0,4},{1,5},{2,6},{3,7},{4,0},{5,1},{6,2},{7,3},{8,12},{9,13},{10,... | collective-permute-start | bytes 49160 | tf_op jit(solution)/shard_map/ppermute | solution.py:300
  17.4 2.6 %collective-permute-start.13 = (s16[4,16,128]{2,1,0:T(8,128)(2,1)S(1)}, s16[4,16,128]{2,1,0:T(8,128)(2,1)S(1)}, u32[]{:S(2)}, u32[]{:S(2)}) collective-permute-start(s16[4,16,128]{2,1,0:T(8,128)(2,1)S(1)} %select_convert_fusion.refs_0_), channel_id=1, source_target_pairs={{0,6},{1,7},{2,4},{3,5},{4,2},{5,3},{6,0},{7,1},{8,14},{9,15},{10,... | collective-permute-start | bytes 49160 | tf_op jit(solution)/shard_map/ppermute | solution.py:300
  20.0 5.4 %collective-permute-start.1 = (bf16[160,512]{1,0:T(8,128)(2,1)}, bf16[160,512]{1,0:T(8,128)(2,1)S(1)}, u32[]{:S(2)}, u32[]{:S(2)}) collective-permute-start(bf16[160,512]{1,0:T(8,128)(2,1)} %refs_0_.1), channel_id=1, source_target_pairs={{0,1},{1,0},{2,3},{3,2},{4,5},{5,4},{6,7},{7,6},{8,9},{9,8},{10,11... | collective-permute-start | bytes 491528 | tf_op jit(solution)/shard_map/ppermute | solution.py:300
  23.5 2.4 %collective-permute-start.3 = (bf16[160,512]{1,0:T(8,128)(2,1)S(1)}, bf16[160,512]{1,0:T(8,128)(2,1)S(1)}, u32[]{:S(2)}, u32[]{:S(2)}) collective-permute-start(bf16[160,512]{1,0:T(8,128)(2,1)S(1)} %collective-permute-done.2.refs_2_), channel_id=1, source_target_pairs={{0,1},{1,0},{2,3},{3,2},{4,5},{5,4},{6,7},{7,6},{8,9},{9,8},{10,11... | collective-permute-start | bytes 491528 | tf_op jit(solution)/shard_map/ppermute | solution.py:300
  23.5 2.5 %collective-permute-start.5 = (bf16[160,512]{1,0:T(8,128)(2,1)S(1)}, bf16[160,512]{1,0:T(8,128)(2,1)S(1)}, u32[]{:S(2)}, u32[]{:S(2)}) collective-permute-start(bf16[160,512]{1,0:T(8,128)(2,1)S(1)} %collective-permute-done.4.refs_4_), channel_id=1, source_target_pairs={{0,1},{1,0},{2,3},{3,2},{4,5},{5,4},{6,7},{7,6},{8,9},{9,8},{10,11... | collective-permute-start | bytes 491528 | tf_op jit(solution)/shard_map/ppermute | solution.py:300
  24.0 5.1 %collective-permute-start.7 = (bf16[160,512]{1,0:T(8,128)(2,1)S(1)}, bf16[160,512]{1,0:T(8,128)(2,1)S(1)}, u32[]{:S(2)}, u32[]{:S(2)}) collective-permute-start(bf16[160,512]{1,0:T(8,128)(2,1)S(1)} %collective-permute-done.6.same), channel_id=1, source_target_pairs={{0,1},{1,0},{2,3},{3,2},{4,5},{5,4},{6,7},{7,6},{8,9},{9,8},{10,11... | collective-permute-start | bytes 491528 | tf_op jit(solution)/shard_map/ppermute | solution.py:300
  25.4 13.2 %collective-permute-start.8 = (s16[4,16,128]{2,1,0:T(8,128)(2,1)S(1)}, s16[4,16,128]{2,1,0:T(8,128)(2,1)S(1)}, u32[]{:S(2)}, u32[]{:S(2)}) collective-permute-start(s16[4,16,128]{2,1,0:T(8,128)(2,1)S(1)} %select_convert_fusion.refs_0_), channel_id=1, source_target_pairs={{0,1},{1,0},{2,3},{3,2},{4,5},{5,4},{6,7},{7,6},{8,9},{9,8},{10,11... | collective-permute-start | bytes 49160 | tf_op jit(solution)/shard_map/ppermute | solution.py:300
  25.9 12.8 %collective-permute-start.10 = (s16[4,16,128]{2,1,0:T(8,128)(2,1)S(1)}, s16[4,16,128]{2,1,0:T(8,128)(2,1)S(1)}, u32[]{:S(2)}, u32[]{:S(2)}) collective-permute-start(s16[4,16,128]{2,1,0:T(8,128)(2,1)S(1)} %collective-permute-done.9.refs_2_), channel_id=1, source_target_pairs={{0,1},{1,0},{2,3},{3,2},{4,5},{5,4},{6,7},{7,6},{8,9},{9,8},{10,11... | collective-permute-start | bytes 49160 | tf_op jit(solution)/shard_map/ppermute | solution.py:300
  26.0 12.7 %collective-permute-start.12 = (s16[4,16,128]{2,1,0:T(8,128)(2,1)S(1)}, s16[4,16,128]{2,1,0:T(8,128)(2,1)S(1)}, u32[]{:S(2)}, u32[]{:S(2)}) collective-permute-start(s16[4,16,128]{2,1,0:T(8,128)(2,1)S(1)} %collective-permute-done.11.refs_4_), channel_id=1, source_target_pairs={{0,1},{1,0},{2,3},{3,2},{4,5},{5,4},{6,7},{7,6},{8,9},{9,8},{10,11... | collective-permute-start | bytes 49160 | tf_op jit(solution)/shard_map/ppermute | solution.py:300
  26.4 12.3 %collective-permute-start.14 = (s16[4,16,128]{2,1,0:T(8,128)(2,1)S(1)}, s16[4,16,128]{2,1,0:T(8,128)(2,1)S(1)}, u32[]{:S(2)}, u32[]{:S(2)}) collective-permute-start(s16[4,16,128]{2,1,0:T(8,128)(2,1)S(1)} %collective-permute-done.13.refs_6_), channel_id=1, source_target_pairs={{0,1},{1,0},{2,3},{3,2},{4,5},{5,4},{6,7},{7,6},{8,9},{9,8},{10,11... | collective-permute-start | bytes 49160 | tf_op jit(solution)/shard_map/ppermute | solution.py:300
  26.5 1.1 %copy-start = (bf16[256,1280]{1,0:T(8,128)(2,1)S(1)}, bf16[256,1280]{1,0:T(8,128)(2,1)}, u32[]{:S(2)}) copy-start(bf16[256,1280]{1,0:T(8,128)(2,1)} %own.5) | copy-start | bytes 1966084
  27.6 0.9 %copy-start.4 = (bf16[160,512]{1,0:T(8,128)(2,1)S(1)}, bf16[160,512]{1,0:T(8,128)(2,1)}, u32[]{:S(2)}) copy-start(bf16[160,512]{1,0:T(8,128)(2,1)} %refs_0_.1) | copy-start | bytes 491524
  30.5 14.2 %all-to-all-start = ((f32[32,4,128]{2,1,0:T(4,128)}), f32[32,4,128]{2,1,0:T(4,128)S(1)}, u32[]{:S(2)}, u32[]{:S(2)}) async-start(f32[32,4,128]{2,1,0:T(4,128)} %get-tuple-element.22), calls=%async_computation | async-start | bytes 131072 | tf_op jit(solution)/shard_map/all_to_all | solution.py:351
  38.6 5.0 %copy-start.1 = (bf16[256,1280]{1,0:T(8,128)(2,1)S(1)}, bf16[256,1280]{1,0:T(8,128)(2,1)}, u32[]{:S(2)}) copy-start(bf16[256,1280]{1,0:T(8,128)(2,1)} %own.5) | copy-start | bytes 1966084
  42.2 1.4 %copy-start.2 = (f32[256,2176]{1,0:T(8,128)}, f32[256,2176]{1,0:T(8,128)S(1)}, u32[]{:S(2)}) copy-start(f32[256,2176]{1,0:T(8,128)S(1)} %shard_map.97.counts) | copy-start | bytes 6684676
  44.7 1.6 %copy-start.3 = (f32[256,2176]{1,0:T(8,128)S(1)}, f32[256,2176]{1,0:T(8,128)}, u32[]{:S(2)}) copy-start(f32[256,2176]{1,0:T(8,128)} %copy-done.2) | copy-start | bytes 6684676
  46.8 1.4 %collective-permute-start.15 = (f32[256,1]{1,0:T(8,128)S(1)}, f32[256,1]{1,0:T(8,128)S(1)}, u32[]{:S(2)}, u32[]{:S(2)}) collective-permute-start(f32[256,1]{1,0:T(8,128)S(1)} %shard_map.98.dscores), channel_id=1, source_target_pairs={{0,1},{1,0},{2,3},{3,2},{4,5},{5,4},{6,7},{7,6},{8,9},{9,8},{10,11... | collective-permute-start | bytes 3080 | tf_op jit(solution)/shard_map/ppermute | solution.py:300
  49.0 4.8 %collective-permute-start.16 = (s16[168,256]{1,0:T(8,128)(2,1)S(1)}, s16[168,256]{1,0:T(8,128)(2,1)S(1)}, u32[]{:S(2)}, u32[]{:S(2)}) collective-permute-start(s16[168,256]{1,0:T(8,128)(2,1)S(1)} %get-tuple-element.31), channel_id=1, source_target_pairs={{0,1},{1,0},{2,3},{3,2},{4,5},{5,4},{6,7},{7,6},{8,9},{9,8},{10,11... | collective-permute-start | bytes 258056 | tf_op jit(solution)/shard_map/ppermute | solution.py:300
  49.4 4.9 %collective-permute-start.17 = (s16[168,256]{1,0:T(8,128)(2,1)S(1)}, s16[168,256]{1,0:T(8,128)(2,1)S(1)}, u32[]{:S(2)}, u32[]{:S(2)}) collective-permute-start(s16[168,256]{1,0:T(8,128)(2,1)S(1)} %get-tuple-element.32), channel_id=1, source_target_pairs={{0,2},{1,3},{2,0},{3,1},{4,6},{5,7},{6,4},{7,5},{8,10},{9,11},{10,... | collective-permute-start | bytes 258056 | tf_op jit(solution)/shard_map/ppermute | solution.py:300
  50.7 5.0 %collective-permute-start.18 = (s16[168,256]{1,0:T(8,128)(2,1)S(1)}, s16[168,256]{1,0:T(8,128)(2,1)S(1)}, u32[]{:S(2)}, u32[]{:S(2)}) collective-permute-start(s16[168,256]{1,0:T(8,128)(2,1)S(1)} %get-tuple-element.33), channel_id=1, source_target_pairs={{0,3},{1,2},{2,1},{3,0},{4,7},{5,6},{6,5},{7,4},{8,11},{9,10},{10,... | collective-permute-start | bytes 258056 | tf_op jit(solution)/shard_map/ppermute | solution.py:300
  51.2 6.5 %collective-permute-start.19 = (s16[168,256]{1,0:T(8,128)(2,1)S(1)}, s16[168,256]{1,0:T(8,128)(2,1)S(1)}, u32[]{:S(2)}, u32[]{:S(2)}) collective-permute-start(s16[168,256]{1,0:T(8,128)(2,1)S(1)} %get-tuple-element.36), channel_id=1, source_target_pairs={{0,4},{1,5},{2,6},{3,7},{4,0},{5,1},{6,2},{7,3},{8,12},{9,13},{10,... | collective-permute-start | bytes 258056 | tf_op jit(solution)/shard_map/ppermute | solution.py:300
  52.7 11.1 %collective-permute-start.20 = (s16[168,256]{1,0:T(8,128)(2,1)S(1)}, s16[168,256]{1,0:T(8,128)(2,1)S(1)}, u32[]{:S(2)}, u32[]{:S(2)}) collective-permute-start(s16[168,256]{1,0:T(8,128)(2,1)S(1)} %get-tuple-element.37), channel_id=1, source_target_pairs={{0,5},{1,4},{2,7},{3,6},{4,1},{5,0},{6,3},{7,2},{8,13},{9,12},{10,... | collective-permute-start | bytes 258056 | tf_op jit(solution)/shard_map/ppermute | solution.py:300
  53.8 13.5 %collective-permute-start.21 = (s16[168,256]{1,0:T(8,128)(2,1)S(1)}, s16[168,256]{1,0:T(8,128)(2,1)S(1)}, u32[]{:S(2)}, u32[]{:S(2)}) collective-permute-start(s16[168,256]{1,0:T(8,128)(2,1)S(1)} %get-tuple-element.38), channel_id=1, source_target_pairs={{0,6},{1,7},{2,4},{3,5},{4,2},{5,3},{6,0},{7,1},{8,14},{9,15},{10,... | collective-permute-start | bytes 258056 | tf_op jit(solution)/shard_map/ppermute | solution.py:300
  54.4 15.0 %collective-permute-start.22 = (s16[168,256]{1,0:T(8,128)(2,1)S(1)}, s16[168,256]{1,0:T(8,128)(2,1)S(1)}, u32[]{:S(2)}, u32[]{:S(2)}) collective-permute-start(s16[168,256]{1,0:T(8,128)(2,1)S(1)} %get-tuple-element.39), channel_id=1, source_target_pairs={{0,7},{1,6},{2,5},{3,4},{4,3},{5,2},{6,1},{7,0},{8,15},{9,14},{10,... | collective-permute-start | bytes 258056 | tf_op jit(solution)/shard_map/ppermute | solution.py:300
